TPU v7x, 256 devices: a whole 4x4x8 slice. The times are simulated.
256 devices in a mesh: rep: 8 (over z), exp: 32 (over x, y, core).
Axes of the slice: x: 4, y: 4, z: 8, core: 2. Of those that a mesh axis runs over, the one named last changes fastest.
Arguments:
- tokens: bfloat16 [4096, 4096], P(('rep', 'exp')), may hold values from -6 to 6
- routed_experts: int32 [4096, 8], P(('rep', 'exp')), may hold values from 0 to 63, all different within a row; in each aligned block of 16 rows (0 to 15, 16 to 31, ...) at most 3 rows name the same one
- route_weights: float32 [4096, 8], P(('rep', 'exp')), may hold values from 0.02 to 0.5
- gate_weight: bfloat16 [64, 1536, 4096], P('exp', 'rep'), may hold values from -0.09375 to 0.09375
- up_weight: bfloat16 [64, 1536, 4096], P('exp', 'rep'), may hold values from -0.09375 to 0.09375
- down_weight: bfloat16 [64, 1536, 4096], P('exp', 'rep'), may hold values from -0.15625 to 0.15625
Outputs:
- layer_output: bfloat16 [4096, 4096], P(('rep', 'exp'))
Inputs may be any that keep to these rules, and one draw needn't show every extreme that they name: `routed_experts`: each token names 8 different experts. Among the 16 tokens of one device (aligned blocks of rows), no expert is named more than 3 times, a bound that some block reaches.
All inputs are finite; a program needn't handle non-finite values.
Results may differ from a plain program's by a relative error of at most 0.01.
Values may be sent and summed in bfloat16 or wider, within the bound.
A program may use at most 128 MiB of HBM per device.

v0:
```python
import jax
import jax.numpy as jnp
from jax import lax
from jax.sharding import PartitionSpec as P


def slot_table(experts, expert_count, capacity):
    blocks = experts.shape[0]
    flattened = experts.reshape(blocks, -1)
    onehot = (
        flattened[:, :, None] == jnp.arange(expert_count, dtype=jnp.int32)[None, None, :]
    ).astype(jnp.int32)
    before = jnp.cumsum(onehot, axis=1) - onehot
    position = jnp.sum(before * onehot, axis=2)
    return flattened * capacity + position


def token_picks(slots, top_count, slot_count):
    blocks = slots.shape[0]
    grouped = slots.reshape(blocks, 1, -1, top_count)
    return jnp.any(grouped == jnp.arange(slot_count, dtype=jnp.int32)[None, :, None, None], axis=3)


def routing_column(route_weights, routed_experts):
    as_float = routed_experts.astype(jnp.float32)
    weights_all, experts_all = (
        lax.all_gather(route_weights, "rep", axis=0, tiled=True),
        lax.all_gather(as_float, "rep", axis=0, tiled=True),
    )
    return (weights_all, experts_all.astype(jnp.int32))


def on_device(tokens, routed_experts, route_weights, gate_weight, up_weight, down_weight):
    replicas = lax.axis_size("rep")
    owners = lax.axis_size("exp")
    token_rows, model_width = tokens.shape
    top_count = routed_experts.shape[1]
    local_experts = gate_weight.shape[0]
    expert_count = local_experts * owners
    capacity = max(2, 3 * token_rows * top_count // (2 * expert_count))
    slot_count = expert_count * capacity
    own_slots = slot_table(routed_experts[None], expert_count, capacity)
    column = None
    column_slots = None
    selected = token_picks(own_slots, top_count, slot_count)[0].astype(jnp.bfloat16)
    buffer = jnp.dot(selected, tokens, preferred_element_type=jnp.float32).astype(jnp.bfloat16)
    buffer = buffer.reshape(owners, local_experts, capacity, model_width)
    arrived = lax.all_to_all(buffer, "exp", split_axis=0, concat_axis=2, tiled=True)
    rows_now = lax.all_gather(arrived, "rep", axis=2, tiled=True)[0]
    gate_value = jnp.einsum(
        "emd,efd->emf", rows_now, gate_weight, preferred_element_type=jnp.float32
    )
    up_value = jnp.einsum("emd,efd->emf", rows_now, up_weight, preferred_element_type=jnp.float32)
    hidden = (jax.nn.silu(gate_value) * up_value).astype(jnp.bfloat16)
    outcome = jnp.einsum("emf,efd->emd", hidden, down_weight, preferred_element_type=jnp.float32)
    outcome = lax.optimization_barrier(outcome.astype(jnp.bfloat16))
    outcomes = outcome[None]
    outcomes = outcomes.reshape(local_experts, replicas, owners, capacity, model_width)
    column = routing_column(route_weights, routed_experts)
    column_slots = slot_table(
        column[1].reshape(replicas, token_rows, top_count), expert_count, capacity
    )
    returned = lax.all_to_all(outcomes, "exp", split_axis=2, concat_axis=0, tiled=True)
    returned = returned.reshape(expert_count, replicas, capacity, model_width)
    expert_index = column_slots // capacity
    place_index = column_slots % capacity
    replica_index = jnp.broadcast_to(
        jnp.arange(replicas, dtype=jnp.int32)[:, None], column_slots.shape
    )
    picked = returned[expert_index, replica_index, place_index].astype(jnp.float32)
    column_weights = column[0].reshape(replicas, token_rows, top_count)
    weighted = jnp.sum(
        picked.reshape(replicas, token_rows, top_count, model_width)
        * column_weights[:, :, :, None],
        axis=2,
    )
    summed = lax.psum_scatter(weighted, "rep", scatter_dimension=0, tiled=True)
    return summed.reshape(token_rows, model_width).astype(jnp.bfloat16)


def solution(mesh):
    placed = (
        P(("rep", "exp"), None),
        P(("rep", "exp"), None),
        P(("rep", "exp"), None),
        P("exp", "rep", None),
        P("exp", "rep", None),
        P("exp", "rep", None),
    )
    return jax.shard_map(
        on_device, mesh=mesh, in_specs=placed, out_specs=P(("rep", "exp"), None), check_vma=False
    )
```

profile of v0, /device:TPU:1, one launch (start us, length us, event | category | flops | bytes accessed | tf_op | source)
XLA Modules:
  0.0 554.5 jit_solution(14770991850050571050)
XLA Ops:
  6.5 0.9 copy.34
  7.4 0.1 eq.65
  7.5 0.1 fusion.25
  7.6 0.2 reduce_window_sum.22
  7.8 0.2 select_reduce_fusion.1
  8.0 0.1 reduce_sum.32
  8.1 0.1 fusion.24
  8.2 2.7 convolution_convert_fusion.1
  10.9 4.1 reshape.225
  15.0 3.6 copy.36
  18.6 31.2 %all_to_all.33 = bf16[32,2,3,4096]{3,1,2,0:T(2,128)(2,1)S(1)} all-to-all(bf16[32,2,3,4096]{3,1,2,0:T(2,128)(2,1)S(1)} %copy.36), channel_id=1, replica_groups=mesh['rep'=8,'exp'=32] {'exp'}, dimensions={0} | all-to-all | bytes 3145728 | tf_op jit(solution)/shard_map/all_to_all | solution.py:48
  49.8 2.1 copy.37
  51.9 132.2 %all-gather.4.cloned.1.call-done = bf16[1,2,768,4096]{3,2,1,0:T(8,128)(2,1)} async-done(((bf16[1,2,96,4096]{3,2,1,0:T(8,128)(2,1)}), bf16[1,2,768,4096]{3,2,1,0:T(8,128)(2,1)}) %all-gather.4.cloned.1.call-update) | async-done | bytes 12582928 | tf_op jit(solution)/shard_map/all_gather | solution.py:49
  184.1 10.8 %fusion.3 = f32[2,768,192]{1,2,0:T(8,128)} fusion(bf16[2,192,4096]{2,1,0:T(8,128)(2,1)} %param.9, bf16[1,2,768,4096]{3,2,1,0:T(8,128)(2,1)} %all-gather.4.cloned.1.call-done), kind=kOutput, calls=%fused_computation.5 | convolution fusion | flops 2415919104 | bytes 16908288 | tf_op jit(solution)/shard_map/emd,efd->emf/dot_general | solution.py:50
  195.0 15.9 %convolution_convert_fusion = bf16[2,768,4096]{2,1,0:T(8,128)(2,1)} fusion(bf16[2,192,4096]{2,1,0:T(8,128)(2,1)S(1)} %copy-done, bf16[2,192,4096]{2,1,0:T(8,128)(2,1)} %param.10, bf16[1,2,768,4096]{3,2,1,0:T(8,128)(2,1)} %all-gather.4.cloned.1.call-done, f32[2,768,192]{1,2,0:T(8,128)} %fusion.3), kind=kOutput, calls=%fused_computation.7 | convolution fusion | flops 4839899136 | bytes 32636928 | tf_op jit(solution)/shard_map/emf,efd->emd/dot_general | solution.py:55
  210.9 21.2 %copy.38 = bf16[2,768,4096]{2,0,1:T(2,128)(2,1)S(1)} copy(bf16[2,768,4096]{2,1,0:T(8,128)(2,1)} %convolution_convert_fusion) | data formatting | bytes 25165824 | tf_op jit(solution)/shard_map/optimization_barrier | solution.py:56
  232.1 11.5 %copy.39 = bf16[2,8,32,3,4096]{4,0,3,1,2:T(2,128)(2,1)} copy(bf16[2,8,32,3,4096]{4,0,3,2,1:T(2,128)(2,1)S(1)} %bitcast.42) | data formatting | bytes 25165824 | tf_op jit(solution)/shard_map/reshape;broadcast_in_dim | solution.py:58
  243.7 7.9 %all-to-all-start.1 = ((bf16[2,8,32,3,4096]{4,0,3,1,2:T(2,128)(2,1)}), bf16[2,8,32,3,4096]{4,0,3,1,2:T(2,128)(2,1)}, u32[]{:S(2)}, u32[]{:S(2)}) async-start(bf16[2,8,32,3,4096]{4,0,3,1,2:T(2,128)(2,1)} %copy.39), calls=%async_computation.1 | async-start | bytes 25165824 | tf_op jit(solution)/shard_map/all_to_all | solution.py:63
  251.6 0.0 reduce-scatter.2.cloned.1.call-start
  251.6 21.1 %all-gather = f32[8,16,8]{1,2,0:T(8,128)S(1)} all-gather(f32[1,16,8]{1,2,0:T(8,128)S(1)} %convert_bitcast_fusion.1), channel_id=1, replica_groups=mesh['rep'=8,'exp'=32] {'rep'}, dimensions={0}, use_global_device_ids=true | all-gather | bytes 4608 | tf_op jit(solution)/shard_map/all_gather | solution.py:28
  272.7 0.1 copy.46
  272.8 2.5 select_reduce_fusion
  275.4 0.1 copy.41
  275.5 0.1 mul.56
  275.6 20.8 %all-gather.1 = f32[8,16,8]{1,2,0:T(8,128)S(1)} all-gather(f32[1,16,8]{1,2,0:T(8,128)S(1)} %bitcast.45), channel_id=1, replica_groups=mesh['rep'=8,'exp'=32] {'rep'}, dimensions={0}, use_global_device_ids=true | all-gather | bytes 4608 | tf_op jit(solution)/shard_map/all_gather | solution.py:27
  296.5 0.1 copy.45
  296.6 130.1 %all-to-all-done.1 = bf16[2,8,32,3,4096]{4,0,3,1,2:T(2,128)(2,1)} async-done(((bf16[2,8,32,3,4096]{4,0,3,1,2:T(2,128)(2,1)}), bf16[2,8,32,3,4096]{4,0,3,1,2:T(2,128)(2,1)}, u32[]{:S(2)}, u32[]{:S(2)}) %all-to-all-start.1) | async-done | bytes 12582944 | tf_op jit(solution)/shard_map/all_to_all | solution.py:63
  426.7 14.5 %copy.40 = bf16[32,2,8,1,3,4096]{5,2,4,1,0,3:T(8,128)(2,1)} copy(bf16[32,2,8,1,3,4096]{5,1,4,2,0,3:T(2,128)(2,1)} %bitcast.6) | data formatting | bytes 25165824 | tf_op jit(solution)/shard_map/all_to_all | solution.py:63
  441.2 34.6 %gather_fusion = bf16[1024,4096]{1,0:T(8,128)(2,1)} fusion(bf16[64,8,3,4096]{3,1,2,0:T(8,128)(2,1)} %bitcast.41, s32[1024]{0:T(1024)S(1)} %fusion.30), kind=kCustom, calls=%fused_computation | custom fusion | bytes 16789504 | tf_op jit(solution)/shard_map/gather | solution.py:70
  475.7 12.9 %fusion = f32[8,16,4096]{2,1,0:T(8,128)} fusion(f32[8,16,8]{2,1,0:T(8,128)S(1)} %copy.45, bf16[1024,4096]{1,0:T(8,128)(2,1)} %gather_fusion), kind=kLoop, calls=%fused_computation.2 | loop fusion | flops 12058624 | bytes 10489856 | tf_op jit(solution)/shard_map/reduce_sum | solution.py:72
  488.7 57.3 %reduce-scatter.2.cloned.1.call-done = f32[1,16,4096]{2,1,0:T(8,128)} async-done(((f32[8,16,4096]{2,1,0:T(8,128)}), f32[1,16,4096]{2,1,0:T(8,128)}) %reduce-scatter.2.cloned.1.call-update) | async-done | bytes 262160 | tf_op jit(solution)/shard_map/reduce_scatter | solution.py:77
  546.0 1.6 convert_bitcast_fusion
  (17 shorter events, 0.2 us)
Async XLA Ops:
  6.5 188.4 %copy-start = (bf16[2,192,4096]{2,1,0:T(8,128)(2,1)S(1)}, bf16[2,192,4096]{2,1,0:T(8,128)(2,1)}, u32[]{:S(2)}) copy-start(bf16[2,192,4096]{2,1,0:T(8,128)(2,1)} %param.11) | copy-start | bytes 9437188
  6.5 177.6 %all-gather.4.cloned.1.call-start = ((), (), s32[]{:S(2)}) async-start(), calls=%async_computation.3 | async-start | bytes 14155776 | tf_op jit(solution)/shard_map/all_gather | solution.py:49
  243.7 7.9 %copy-start.2 = (s32[16,8]{0,1:T(8,128)S(1)}, s32[16,8]{0,1:T(8,128)}, u32[]{:S(2)}) copy-start(s32[16,8]{0,1:T(8,128)} %param.7) | copy-start | bytes 1540
  243.7 31.9 %copy-start.3 = (f32[16,8]{0,1:T(8,128)S(1)}, f32[16,8]{0,1:T(8,128)}, u32[]{:S(2)}) copy-start(f32[16,8]{0,1:T(8,128)} %param.8) | copy-start | bytes 1540
  243.7 183.0 %all-to-all-start.1 = ((bf16[2,8,32,3,4096]{4,0,3,1,2:T(2,128)(2,1)}), bf16[2,8,32,3,4096]{4,0,3,1,2:T(2,128)(2,1)}, u32[]{:S(2)}, u32[]{:S(2)}) async-start(bf16[2,8,32,3,4096]{4,0,3,1,2:T(2,128)(2,1)} %copy.39), calls=%async_computation.1 | async-start | bytes 25165824 | tf_op jit(solution)/shard_map/all_to_all | solution.py:63
  251.6 294.5 %reduce-scatter.2.cloned.1.call-start = ((), (), s32[]{:S(2)}) async-start(), calls=%async_computation.4 | async-start | bytes 2359296 | tf_op jit(solution)/shard_map/reduce_scatter | solution.py:77
  475.7 71.9 %copy-start.1 = (bf16[2,192,4096]{2,1,0:T(8,128)(2,1)S(1)}, bf16[2,192,4096]{2,1,0:T(8,128)(2,1)}, u32[]{:S(2)}) copy-start(bf16[2,192,4096]{2,1,0:T(8,128)(2,1)} %param.11) | copy-start | bytes 9437188
Sparse Core Ops, SparseCore 0:
  52.0 132.0 all-gather.3
  488.8 57.1 reduce-scatter.1
where the time goes:
time: 559 us; the launch traced here: 555 us
  waiting for transfers between devices  320 us (57%)
  local copies, waits for them, and re-layouts  93.1 us (17%)
  blocking collectives  73.1 us (13%)
  matrix products  29.5 us (5%)
  other arithmetic  17.7 us (3%)
  between operations  13.5 us (2%)
  starting transfers between devices  7.92 us (1%)
    all_gather x1, waiting for transfers between devices, on_device(): rows_now = lax.all_gather(arrived, 'rep', axis=2, tiled=True)[0]  132 us
    all_to_all x1, waiting for transfers between devices, on_device(): lax.all_to_all(outcomes, 'exp', split_axis=2, concat_axis=0, tiled=True)  130 us
    reduce_scatter x1, waiting for transfers between devices, on_device(): summed = lax.psum_scatter(weighted, 'rep', scatter_dimension=0, tiled=True)  57.3 us
    gather x1, local copies, waits for them, and re-layouts, on_device(): returned[expert_index, replica_index, place_index].astype(jnp.float32)  34.6 us
    all_to_all x1, blocking collectives, on_device(): lax.all_to_all(buffer, 'exp', split_axis=0, concat_axis=2, tiled=True)  31.2 us
    optimization_barrier x1, local copies, waits for them, and re-layouts, on_device(): outcome = lax.optimization_barrier(outcome.astype(jnp.bfloat16))  21.2 us
    all_gather x1, blocking collectives, routing_column(): lax.all_gather(as_float, 'rep', axis=0, tiled=True)  21.1 us
    all_gather x1, blocking collectives, routing_column(): lax.all_gather(route_weights, 'rep', axis=0, tiled=True)  20.8 us
  transfers between devices with their start and end apart: 3, of which 3 were waited for; matrix products, arithmetic and copies ran while one was open for 1% of the time, Pallas kernels for 0%

commit v1 on v0

v1 whole, which is shorter than its diff:
```python
import heapq

import jax
import jax.numpy as jnp
from jax import lax
from jax.experimental import pallas as pl
from jax.experimental.pallas import tpu as pltpu
from jax.sharding import PartitionSpec as P

MESH = pl.DeviceIdType.MESH
LANES = 128
CAPACITY = 3
GROUPS_PER_CHUNK = 4
RATE = 46000.0
LATENCY = 1.8
ORDERS = ((0, 1, 2), (0, 2, 1), (1, 2, 0))
ROWS = 32


def half_steps(size):
    middle = size // 2
    found = []
    for direction in (1, -1):
        first, second = (0, 1) if direction == 1 else (1, 0)
        for step in range(1, middle + 1):
            if step == middle:
                found.append((direction, step, first))
            else:
                found.append((direction, step, first))
                found.append((direction, step, second))
    return found


def reduce_steps(size):
    middle = size // 2
    found = []
    for direction in (1, -1):
        first, second = (0, 1) if direction == 1 else (1, 0)
        for step in range(1, middle + 1):
            if step == 1:
                found.append((direction, step, first))
            else:
                found.append((direction, step, second))
                found.append((direction, step, first))
    return found


def simulate(copies):
    waiting = {key: set(value[2]) for key, value in copies.items()}
    readers = {}
    for key, value in copies.items():
        for other in value[2]:
            readers.setdefault(other, []).append(key)
    free = {}
    serial = 0
    heap = []
    for key in copies:
        if not waiting[key]:
            heap.append((0.0, serial, "start", key))
            serial += 1
    heapq.heapify(heap)
    order = []
    while heap:
        now, _, kind, key = heapq.heappop(heap)
        order.append((kind, key, now))
        link, size, _, delay = copies[key]
        if kind == "start":
            done = max(now, free.get(link, 0.0)) + size / RATE
            free[link] = done
            heapq.heappush(heap, (done + LATENCY, serial, "arrive", key))
            serial += 1
        else:
            for reader in readers.get(key, []):
                waiting[reader].discard(key)
                if not waiting[reader]:
                    heapq.heappush(heap, (now + delay, serial, "start", reader))
                    serial += 1
    return order


def gather_plan(sizes, widths):
    copies = {}
    for color, order in enumerate(ORDERS):
        per_block = ROWS * widths[color] * 2
        for stage in range(3):
            axis = order[stage]
            block = per_block
            for earlier in order[:stage]:
                block *= sizes[earlier]
            for direction, step, half in half_steps(sizes[axis]):
                if step > 1:
                    needs = {(color, stage, direction, step - 1, half)}
                elif stage == 0:
                    needs = set()
                else:
                    needs = set()
                    for d, s, h in half_steps(sizes[order[stage - 1]]):
                        if stage == 1 or h == half:
                            needs.add((color, stage - 1, d, s, h))
                key = (color, stage, direction, step, half)
                copies[key] = ((axis, direction), block / 2, needs, 0.0)
    return copies


def reduce_plan(sizes, widths):
    copies = {}
    for color, order in enumerate(ORDERS):
        per_block = ROWS * widths[color] * 2
        for stage in (2, 1, 0):
            axis = order[stage]
            block = per_block
            for earlier in order[:stage]:
                block *= sizes[earlier]
            last = sizes[axis] // 2
            for direction, step, half in reduce_steps(sizes[axis]):
                needs = set()
                first = 0 if direction == 1 else 1
                if step > 2 or (step == 2 and half == first):
                    needs.add((color, stage, direction, step - 1, half))
                elif stage < 2:
                    above = sizes[order[stage + 1]]
                    for d, s, h in reduce_steps(above):
                        if s == above // 2 and (stage == 0 or h == half):
                            needs.add((color, stage + 1, d, s, h))
                key = (color, stage, direction, step, half)
                copies[key] = ((axis, direction), block / 2, needs, block / 2 / 2e6)
    return copies


def make_kernel(sizes, widths, half_width, experts_here, spe):
    groups_x = 2
    nz, nx, ny = sizes
    group_tokens = groups_x * ny * ROWS
    slots = experts_here * spe
    groups = nz * (nx // groups_x)
    per_chunk = min(GROUPS_PER_CHUNK, groups)
    chunks = groups // per_chunk
    offsets = (0, widths[0], widths[0] + widths[1])
    gather_widths = (widths[0] + LANES, widths[1], widths[2])
    gather = gather_plan(sizes, gather_widths)
    gather_order = simulate(gather)
    gather_number = {key: n for n, key in enumerate(gather)}
    reduce = reduce_plan(sizes, widths)
    reduce_order = simulate(reduce)
    reduce_number = {key: n for n, key in enumerate(reduce)}
    buffers = {}
    buffer_of = {}
    for color, order in enumerate(ORDERS):
        for stage in range(3):
            steps = reduce_steps(sizes[order[stage]])
            earlier = [sizes[a] for a in sorted(order[:stage])]
            if stage == 0:
                shape = (ROWS // 2, widths[color])
            else:
                shape = []
                for a in sorted(order[:stage]):
                    shape.append(sizes[a] // 2 if a == order[0] else sizes[a])
                shape = tuple(shape) + (ROWS, widths[color])
            buffers[(color, stage)] = (len(steps),) + shape
            for n, step in enumerate(steps):
                buffer_of[(color, stage) + step] = n
    buffer_keys = sorted(buffers)

    def kernel(
        x_ref, table_ref, pick_ref, weigh_ref, code_ref, code_t_ref, gate_hbm, up_hbm, down_hbm,
        out_ref, g0, g1, g2, gate_up, down, chosen, pre, pre_out, pre_in, fin_out, fin_in,
        *rest,
    ):
        landing = dict(zip(buffer_keys, rest[: len(buffer_keys)]))
        (own_sem, pair_send, pair_recv, load_sem, load_send, load_recv,
         gather_send, gather_recv, reduce_send, reduce_recv,
         pre_send, pre_recv, fin_send, fin_recv) = rest[len(buffer_keys):]
        held = (g0, g1, g2)
        z = lax.axis_index("rep")
        e = lax.axis_index("exp")
        core = lax.rem(e, 2)
        chip = lax.div(e, 2)
        y = lax.rem(chip, ny)
        x = lax.div(chip, ny)
        here = (z, x, y)
        partner = (z, e + 1 - 2 * core)

        def neighbour(axis, direction):
            moved = list(here)
            moved[axis] = lax.rem(here[axis] + direction + sizes[axis], sizes[axis])
            return (moved[0], (moved[1] * ny + moved[2]) * 2 + core)

        barrier = pltpu.get_barrier_semaphore()
        peers = [partner] + [neighbour(a, d) for a in range(3) for d in (1, -1)]
        for peer in peers:
            pl.semaphore_signal(barrier, inc=1, device_id=peer, device_id_type=MESH)
        pl.semaphore_wait(barrier, len(peers))

        def block(color, stage, index, half, width):
            order = ORDERS[color]
            where = []
            for a in range(3):
                if a == order[stage]:
                    where.append(index)
                elif a in order[:stage]:
                    if a == order[0]:
                        where.append(pl.ds(half * (sizes[a] // 2), sizes[a] // 2))
                    else:
                        where.append(pl.ds(0, sizes[a]))
                else:
                    where.append(here[a])
            rows = pl.ds(half * (ROWS // 2), ROWS // 2) if stage == 0 else pl.ds(0, ROWS)
            return held[color].at[where[0], where[1], where[2], rows, pl.ds(0, width)]

        own_rows = pl.ds(pl.multiple_of(core * 16, 16), 16)
        own_copies, pair_copies = [], []
        for color in range(3):
            for mine in (True, False):
                side = core if mine else 1 - core
                start = pl.multiple_of(side * half_width + offsets[color], LANES)
                source = x_ref.at[:, pl.ds(start, widths[color])]
                target = held[color].at[z, x, y, own_rows, pl.ds(0, widths[color])]
                if mine:
                    own_copies.append(
                        pltpu.make_async_copy(source, target, own_sem.at[color])
                    )
                else:
                    pair_copies.append(
                        pltpu.make_async_remote_copy(
                            src_ref=source, dst_ref=target, send_sem=pair_send.at[color],
                            recv_sem=pair_recv.at[color], device_id=partner,
                            device_id_type=MESH,
                        )
                    )
        table_target = g0.at[z, x, y, own_rows, pl.ds(widths[0], LANES)]
        own_copies.append(pltpu.make_async_copy(table_ref, table_target, own_sem.at[3]))
        pair_copies.append(
            pltpu.make_async_remote_copy(
                src_ref=table_ref, dst_ref=table_target, send_sem=pair_send.at[3],
                recv_sem=pair_recv.at[3], device_id=partner, device_id_type=MESH,
            )
        )
        for copy in pair_copies:
            copy.start()
        for copy in own_copies:
            copy.start()

        local = experts_here // 2
        mine_experts = pl.ds(core * local, local)
        load_copies, send_copies = [], []
        for n, (source, target) in enumerate(
            (
                (gate_hbm, gate_up.at[mine_experts, 0]),
                (up_hbm, gate_up.at[mine_experts, 1]),
                (down_hbm, down.at[mine_experts]),
            )
        ):
            start = pl.multiple_of(core * half_width, LANES)
            other = pl.multiple_of((1 - core) * half_width, LANES)
            load_copies.append(
                pltpu.make_async_copy(
                    source.at[:, :, pl.ds(start, half_width)], target, load_sem.at[n]
                )
            )
            send_copies.append(
                pltpu.make_async_remote_copy(
                    src_ref=source.at[:, :, pl.ds(other, half_width)], dst_ref=target,
                    send_sem=load_send.at[n], recv_sem=load_recv.at[n], device_id=partner,
                    device_id_type=MESH,
                )
            )
        for copy in own_copies:
            copy.wait()
        for copy in pair_copies:
            copy.wait()
        for copy in load_copies:
            copy.start()
        for copy in send_copies:
            copy.start()

        def gather_copy(key, received):
            color, stage, direction, step, half = key
            axis = ORDERS[color][stage]
            back = step if received else step - 1
            index = lax.rem(here[axis] - direction * back + sizes[axis], sizes[axis])
            place = block(color, stage, index, half, gather_widths[color])
            n = gather_number[key]
            return pltpu.make_async_remote_copy(
                src_ref=place, dst_ref=place, send_sem=gather_send.at[n],
                recv_sem=gather_recv.at[n], device_id=neighbour(axis, direction),
                device_id_type=MESH,
            )

        for kind, key, _ in gather_order:
            if kind == "start":
                gather_copy(key, False).start()
            else:
                gather_copy(key, True).wait_recv()
        for key in gather:
            gather_copy(key, False).wait_send()
        for copy in load_copies:
            copy.wait()
        for copy in send_copies:
            copy.wait()

        def contract_last(a, b):
            return lax.dot_general(
                a, b, (((1,), (1,)), ((), ())), preferred_element_type=jnp.float32
            )

        def group_place(number):
            gz = lax.div(number, nx // groups_x)
            gx = lax.rem(number, nx // groups_x) * groups_x
            return gz, pl.ds(gx, groups_x)

        def group_table(gz, gx):
            return g0[gz, gx, :, :, pl.ds(widths[0], LANES)].reshape(group_tokens, LANES)

        def pre_copy(q):
            return pltpu.make_async_remote_copy(
                src_ref=pre_out.at[q], dst_ref=pre_in.at[q], send_sem=pre_send.at[q],
                recv_sem=pre_recv.at[q], device_id=partner, device_id_type=MESH,
            )

        def first_half(q, carry):
            def select(g, inner):
                gz, gx = group_place(q * per_chunk + g)
                codes = contract_last(pick_ref[...], group_table(gz, gx))
                onehot = (codes == code_ref[...]).astype(jnp.bfloat16)
                for color in range(3):
                    rows = held[color][gz, gx, :, :, pl.ds(0, widths[color])]
                    rows = rows.reshape(group_tokens, widths[color])
                    picked = jnp.dot(onehot, rows, preferred_element_type=jnp.float32)
                    picked = picked.astype(jnp.bfloat16)
                    for n in range(experts_here):
                        chosen[n, pl.ds(pl.multiple_of(g * spe, 16), spe),
                               pl.ds(offsets[color], widths[color])] = (
                            picked[n * spe:(n + 1) * spe]
                        )
                return inner

            lax.fori_loop(0, per_chunk, select, 0)

            def project(n, inner):
                for which in range(2):
                    value = contract_last(chosen[n], gate_up[n, which])
                    pre[q, n, which] = value
                    pre_out[q, n, which] = value.astype(jnp.bfloat16)
                return inner

            lax.fori_loop(0, experts_here, project, 0)
            pre_copy(q).start()
            return carry

        lax.fori_loop(0, chunks, first_half, 0)

        def second_half(q, carry):
            pre_copy(q).wait_recv()

            def expand(n, inner):
                gate_value = pre[q, n, 0] + pre_in[q, n, 0].astype(jnp.float32)
                up_value = pre[q, n, 1] + pre_in[q, n, 1].astype(jnp.float32)
                hidden = gate_value / (1.0 + jnp.exp(-gate_value)) * up_value
                outcome = jnp.dot(
                    hidden.astype(jnp.bfloat16), down[n], preferred_element_type=jnp.float32
                ).astype(jnp.bfloat16)
                for g in range(per_chunk):
                    chosen[g, pl.ds(pl.multiple_of(n * spe, 16), spe)] = (
                        outcome[g * spe:(g + 1) * spe]
                    )
                return inner

            lax.fori_loop(0, experts_here, expand, 0)

            def combine(g, inner):
                gz, gx = group_place(q * per_chunk + g)
                table = group_table(gz, gx)
                codes = contract_last(table, pick_ref[...])
                weights = contract_last(table, weigh_ref[...])
                scatter = jnp.where(codes == code_t_ref[...], weights, 0.0).astype(jnp.bfloat16)
                for color in range(3):
                    part = chosen[g, :, pl.ds(offsets[color], widths[color])]
                    summed = jnp.dot(scatter, part, preferred_element_type=jnp.float32)
                    held[color][gz, gx, :, :, pl.ds(0, widths[color])] = summed.astype(
                        jnp.bfloat16
                    ).reshape(groups_x, ny, ROWS, widths[color])
                return inner

            lax.fori_loop(0, per_chunk, combine, 0)
            pre_copy(q).wait_send()
            return carry

        lax.fori_loop(0, chunks, second_half, 0)

        def reduce_copy(key):
            color, stage, direction, step, half = key
            axis = ORDERS[color][stage]
            size = sizes[axis]
            index = lax.rem(here[axis] + direction * (size // 2 - step + 1) + size, size)
            n = reduce_number[key]
            return pltpu.make_async_remote_copy(
                src_ref=block(color, stage, index, half, widths[color]),
                dst_ref=landing[(color, stage)].at[buffer_of[key]],
                send_sem=reduce_send.at[n], recv_sem=reduce_recv.at[n],
                device_id=neighbour(axis, direction), device_id_type=MESH,
            )

        def add_into(target, sources):
            lead = target.shape[:-2]
            if not lead:
                total = target[...].astype(jnp.float32)
                for source in sources:
                    total = total + source[...].astype(jnp.float32)
                target[...] = total.astype(jnp.bfloat16)
                return
            inner_size = lead[1] if len(lead) > 1 else 1

            def one(n, carry):
                if len(lead) == 1:
                    where = (n,)
                else:
                    where = (lax.div(n, inner_size), lax.rem(n, inner_size))
                total = target[where].astype(jnp.float32)
                for source in sources:
                    total = total + source[where].astype(jnp.float32)
                target[where] = total.astype(jnp.bfloat16)
                return carry

            lax.fori_loop(0, lead[0] * inner_size, one, 0)

        arrived = set()
        for kind, key, _ in reduce_order:
            if kind == "start":
                reduce_copy(key).start()
                continue
            reduce_copy(key).wait_recv()
            arrived.add(key)
            color, stage, direction, step, half = key
            axis = ORDERS[color][stage]
            size = sizes[axis]
            last = size // 2
            if step < last:
                index = lax.rem(here[axis] + direction * (last - step) + size, size)
                target = block(color, stage, index, half, widths[color])
                add_into(target, [landing[(color, stage)].at[buffer_of[key]]])
                continue
            parts = [
                k for k in reduce
                if k[0] == color and k[1] == stage and k[3] == last and k[4] == half
            ]
            if all(k in arrived for k in parts):
                target = block(color, stage, here[axis], half, widths[color])
                add_into(target, [landing[(color, stage)].at[buffer_of[k]] for k in parts])

        other_rows = pl.ds(pl.multiple_of((1 - core) * 16, 16), 16)
        for color in range(3):
            columns = pl.ds(offsets[color], widths[color])
            fin_out[:, columns] = held[color][z, x, y, other_rows, pl.ds(0, widths[color])]
        last_copy = pltpu.make_async_remote_copy(
            src_ref=fin_out, dst_ref=fin_in, send_sem=fin_send, recv_sem=fin_recv,
            device_id=partner, device_id_type=MESH,
        )
        last_copy.start()
        for color in range(3):
            start = pl.multiple_of(core * half_width + offsets[color], LANES)
            out_ref[:, pl.ds(start, widths[color])] = held[color][
                z, x, y, own_rows, pl.ds(0, widths[color])
            ]
        for key in reduce:
            reduce_copy(key).wait_send()
        last_copy.wait()
        out_ref[:, pl.ds(pl.multiple_of((1 - core) * half_width, LANES), half_width)] = fin_in[...]

    shared = dict(
        gather=len(gather), reduce=len(reduce), chunks=chunks, per_chunk=per_chunk,
        gather_widths=gather_widths, buffers=[buffers[k] for k in buffer_keys],
        group_tokens=group_tokens, slots=slots,
    )
    return kernel, shared


def routing_table(routed_experts, route_weights, expert_count):
    onehot = routed_experts[:, :, None] == jnp.arange(expert_count, dtype=jnp.int32)
    named = jnp.any(onehot, axis=1).astype(jnp.float32)
    rank = jnp.cumsum(named, axis=0)
    weights = jnp.sum(jnp.where(onehot, route_weights[:, :, None], 0.0), axis=1)
    table = jnp.concatenate([named * rank, weights], axis=1)
    pad = LANES - table.shape[1]
    return jnp.pad(table, ((0, 0), (0, pad))).astype(jnp.bfloat16)


def solution(mesh):
    nz = mesh.shape["rep"]
    nx = int(round((mesh.shape["exp"] // 2) ** 0.5))
    ny = mesh.shape["exp"] // 2 // nx
    sizes = (nz, nx, ny)

    def on_device(tokens, routed_experts, route_weights, gate_weight, up_weight, down_weight):
        token_rows, width = tokens.shape
        local, units = gate_weight.shape[:2]
        expert_count = local * mesh.shape["exp"]
        experts_here = 2 * local
        half_width = width // 2
        tiles = half_width // LANES
        thin = max(1, 5 * tiles // 16) * LANES
        widths = (thin, thin, half_width - 2 * thin)
        spe = CAPACITY * (2 * ny * ROWS // token_rows)
        kernel, info = make_kernel(sizes, widths, half_width, experts_here, spe)
        slots, group_tokens = info["slots"], info["group_tokens"]
        chunks, per_chunk = info["chunks"], info["per_chunk"]

        table = routing_table(routed_experts, route_weights, expert_count)
        chip = lax.axis_index("exp") // 2
        slot = jnp.arange(slots, dtype=jnp.int32)
        lane = jnp.arange(LANES, dtype=jnp.int32)
        expert_of = chip * experts_here + slot // spe
        pick = (lane[None, :] == expert_of[:, None]).astype(jnp.bfloat16)
        weigh = (lane[None, :] == expert_of[:, None] + expert_count).astype(jnp.bfloat16)
        block_of_token = jnp.arange(group_tokens, dtype=jnp.int32) // token_rows
        block_of_slot = (slot % spe) // CAPACITY
        code = jnp.where(
            block_of_slot[:, None] == block_of_token[None, :], (slot % CAPACITY + 1)[:, None], -1
        ).astype(jnp.float32)

        bf16 = jnp.bfloat16
        dma = pltpu.SemaphoreType.DMA
        vmem = pl.BlockSpec(memory_space=pltpu.VMEM)
        hbm = pl.BlockSpec(memory_space=pl.ANY)
        return pl.pallas_call(
            kernel,
            out_shape=jax.ShapeDtypeStruct((token_rows, width), bf16),
            in_specs=[vmem] * 6 + [hbm] * 3,
            out_specs=vmem,
            scratch_shapes=[
                *[pltpu.VMEM((nz, nx, ny, ROWS, w), bf16) for w in info["gather_widths"]],
                pltpu.VMEM((experts_here, 2, units, half_width), bf16),
                pltpu.VMEM((experts_here, units, half_width), bf16),
                pltpu.VMEM((max(experts_here, per_chunk), max(slots, per_chunk * spe), half_width), bf16),
                pltpu.VMEM((chunks, experts_here, 2, per_chunk * spe, units), jnp.float32),
                pltpu.VMEM((chunks, experts_here, 2, per_chunk * spe, units), bf16),
                pltpu.VMEM((chunks, experts_here, 2, per_chunk * spe, units), bf16),
                pltpu.VMEM((token_rows, half_width), bf16),
                pltpu.VMEM((token_rows, half_width), bf16),
                *[pltpu.VMEM(shape, bf16) for shape in info["buffers"]],
                dma((4,)), dma((4,)), dma((4,)), dma((3,)), dma((3,)), dma((3,)),
                dma((info["gather"],)), dma((info["gather"],)),
                dma((info["reduce"],)), dma((info["reduce"],)),
                dma((chunks,)), dma((chunks,)), dma(()), dma(()),
            ],
            compiler_params=pltpu.CompilerParams(
                collective_id=0, has_side_effects=True, vmem_limit_bytes=67_000_000
            ),
        )(tokens, table, pick, weigh, code, code.T, gate_weight, up_weight, down_weight)

    placed = (
        P(("rep", "exp"), None),
        P(("rep", "exp"), None),
        P(("rep", "exp"), None),
        P("exp", "rep", None),
        P("exp", "rep", None),
        P("exp", "rep", None),
    )
    return jax.shard_map(
        on_device, mesh=mesh, in_specs=placed, out_specs=P(("rep", "exp"), None), check_vma=False
    )
```

time: 559 us -> 218 us (0.39)
  waiting for transfers between devices: 320 us -> 0 us
  Pallas kernels: 0 us -> 210 us
  local copies, waits for them, and re-layouts: 93.1 us -> 3.09 us
  blocking collectives: 73.1 us -> 0 us
  matrix products: 29.5 us -> 0 us
  other arithmetic: 17.7 us -> 4 us
  between operations: 13.5 us -> 0.02 us
  starting transfers between devices: 7.92 us -> 0 us
    pallas_call x0 -> x1, Pallas kernels: none -> 210 us  [on_device(): pl.pallas_call(kernel, out_shape=jax.ShapeDtypeStruct((token_rows, width)...]
    all_gather x1 -> x0, waiting for transfers between devices: 132 us -> none  [on_device(): rows_now = lax.all_gather(arrived, 'rep', axis=2, tiled=True)[0]]
    all_to_all x1 -> x0, waiting for transfers between devices: 130 us -> none  [on_device(): lax.all_to_all(outcomes, 'exp', split_axis=2, concat_axis=0, tiled=True)]
    reduce_scatter x1 -> x0, waiting for transfers between devices: 57.3 us -> none  [on_device(): summed = lax.psum_scatter(weighted, 'rep', scatter_dimension=0, tiled=True)]
    all_gather x2 -> x0, blocking collectives: 41.9 us -> none  [the longest x1 21.1 us: routing_column(): lax.all_gather(as_float, 'rep', axis=0, tiled=True)]
    gather x1 -> x0, local copies, waits for them, and re-layouts: 34.6 us -> none  [on_device(): returned[expert_index, replica_index, place_index].astype(jnp.float32)]
    all_to_all x1 -> x0, blocking collectives: 31.2 us -> none  [on_device(): lax.all_to_all(buffer, 'exp', split_axis=0, concat_axis=2, tiled=True)]
    dot_general x3 -> x0, matrix products: 29.5 us -> none  [the longest x1 15.9 us: on_device(): jnp.einsum('emf,efd->emd', hidden, down_weight, preferred_element_type=jn...]
  transfers between devices with their start and end apart: 3 -> 0, of which waited for: 3 -> 0; matrix products, arithmetic and copies ran while one was open for 1% -> 0% of each run, Pallas kernels for 0% -> 0%
where the time goes in v1:
time: 218 us
  Pallas kernels  210 us (96%)
  other arithmetic  4 us (2%)
  local copies, waits for them, and re-layouts  3.09 us (1%)
    pallas_call x1, Pallas kernels, on_device(): pl.pallas_call(kernel, out_shape=jax.ShapeDtypeStruct((token_rows, width)...  210 us

profile of v1, /device:TPU:1, one launch (start us, length us, event | category | flops | bytes accessed | tf_op | source)
XLA Modules:
  0.0 217.5 jit_solution(17787157201331791337)
XLA Ops:
  0.0 0.8 copy.9
  0.8 0.1 fusion.2
  1.0 0.8 copy.10
  1.7 0.1 select_reduce_fusion
  1.8 0.7 pad_maximum_fusion.table_ref
  2.5 0.7 fusion.pick_ref
  3.2 0.7 fusion.1.weigh_ref
  3.9 0.8 select_convert_fusion.1.code_ref
  4.7 0.8 select_convert_fusion.code_t_ref
  5.5 210.4 %shard_map.64 = bf16[16,4096]{1,0:T(8,128)(2,1)} custom-call(bf16[16,4096]{1,0:T(8,128)(2,1)} %x_ref.1, bf16[16,128]{1,0:T(8,128)(2,1)} %pad_maximum_fusion.table_ref, bf16[192,128]{1,0:T(8,128)(2,1)} %fusion.pick_ref, bf16[192,128]{1,0:T(8,128)(2,1)} %fusion.1.weigh_ref, f32[192,256]{1,0:T(8,128)} %select_convert_fusion.1.code_ref, ...), custom_call_target="tpu_custom_call" | custom-call | tf_op jit(solution)/shard_map/pallas_call | solution.py:524
  215.9 1.6 copy.12
  (6 shorter events, 0.1 us)

commit v2 on v0

v2 whole, which is shorter than its diff:
```python
import heapq

import jax
import jax.numpy as jnp
import numpy as np
from jax import lax
from jax.experimental import pallas as pl
from jax.experimental.pallas import tpu as pltpu
from jax.sharding import PartitionSpec as P

MESH = pl.DeviceIdType.MESH
LANES = 128
CAPACITY = 3
PHASES = 2
HALVES = 2
ORDERS = ((0, 1, 2), (0, 2, 1), (1, 2, 0))
LONG = (1, -1, 1)
RATE = 46000.0
PAIR_RATE = 150000.0
LATENCY = 1.8
LOOK = 4.0
ADD_RATE = 1.5e6
COSTS = {"select": 0.85, "project": 2.5, "expand": 1.9, "combine": 1.9}


def steps_of(size, split, long, gathering):
    middle = size // 2
    odd_step = middle if gathering else 1
    found = []
    for step in range(1, middle + 1):
        for direction in (1, -1):
            if split:
                first = 0 if direction == 1 else 1
                both = (first, 1 - first) if gathering else (1 - first, first)
                for half in both:
                    if step != odd_step or half == first:
                        found.append((direction, step, half))
            elif step != odd_step or direction == long:
                found.append((direction, step, 0))
    return found


def block_bytes(sizes, width, rows, order, stage):
    total = rows * width * 2
    for axis in order[:stage]:
        total *= sizes[axis]
    return total // 2 if stage else total


def build_tasks(sizes, gather_widths, reduce_widths, rows, exchange_bytes):
    tasks = {}
    chunk_before = None
    for p in range(PHASES):
        arrivals = {}
        for c, order in enumerate(ORDERS):
            for stage in range(3):
                axis = order[stage]
                for d, s, h in steps_of(sizes[axis], stage > 0, LONG[c], True):
                    if s > 1:
                        needs = {("g", p, c, stage, d, s - 1, h)}
                    elif stage == 0:
                        needs = set()
                    else:
                        needs = {
                            k for k in tasks
                            if k[:4] == ("g", p, c, stage - 1) and (stage == 1 or k[6] == h)
                        }
                    key = ("g", p, c, stage, d, s, h)
                    size = block_bytes(sizes, gather_widths[p][c], rows, order, stage)
                    tasks[key] = ((axis, d), size, needs)
            arrivals[c] = {k for k in tasks if k[:4] == ("g", p, c, 2)}
        for q in range(HALVES):
            for c in range(3):
                needs = set(arrivals[2])
                if c < 2:
                    needs |= {k for k in arrivals[c] if k[6] == q}
                if chunk_before is not None:
                    needs.add(("project",) + chunk_before)
                tasks[("select", p, q, c)] = (None, COSTS["select"], needs)
            tasks[("project", p, q)] = (
                None, COSTS["project"], {("select", p, q, c) for c in range(3)}
            )
            tasks[("x", p, q)] = (("pair", 0), exchange_bytes, {("project", p, q)})
            needs = {("x", p, q)}
            if chunk_before is not None:
                needs.add(("combine",) + chunk_before)
            tasks[("expand", p, q)] = (None, COSTS["expand"], needs)
            tasks[("combine", p, q)] = (None, COSTS["combine"], {("expand", p, q)})
            chunk_before = (p, q)
        for c, order in enumerate(ORDERS):
            for stage in (2, 1, 0):
                axis = order[stage]
                steps = steps_of(sizes[axis], stage > 0, LONG[c], False)
                for d, s, h in steps:
                    if (d, s - 1, h) in steps:
                        needs = {("r", p, c, stage, d, s - 1, h)}
                    elif stage == 2:
                        needs = {("combine", p, q) for q in range(HALVES) if c == 2 or q == h}
                    else:
                        needs = {
                            k for k in tasks
                            if k[:4] == ("r", p, c, stage + 1)
                            and k[5] == sizes[order[stage + 1]] // 2
                            and (stage == 0 or k[6] == h)
                        }
                    key = ("r", p, c, stage, d, s, h)
                    size = block_bytes(sizes, reduce_widths[p][c], rows, order, stage)
                    tasks[key] = ((axis, d), size, needs)
    return tasks


def priority(key):
    if key[0] == "g":
        return key[1] * 10 + key[3]
    if key[0] == "r":
        return 20 + key[1] * 10 + key[3]
    return key[1] + {"select": 40, "project": 40, "x": 0, "expand": 10, "combine": 10}[key[0]]


def schedule(tasks):
    waiting = {k: set(v[2]) for k, v in tasks.items()}
    readers = {}
    for k, v in tasks.items():
        for other in v[2]:
            readers.setdefault(other, []).append(k)
    place = {k: n for n, k in enumerate(tasks)}
    free, pending, arriving, computing, order = {}, {}, [], [], []
    now = 0.0

    def ready(k):
        link = tasks[k][0]
        queue = computing if link is None else pending.setdefault(link, [])
        heapq.heappush(queue, (priority(k), place[k], k))

    def pump():
        for link, queue in pending.items():
            while queue and free.get(link, 0.0) - now < LOOK:
                k = heapq.heappop(queue)[2]
                order.append(("start", k))
                rate = PAIR_RATE if link[0] == "pair" else RATE
                free[link] = max(now, free.get(link, 0.0)) + tasks[k][1] / rate
                heapq.heappush(arriving, (free[link] + LATENCY, place[k], k))

    def finish(k):
        for reader in readers.get(k, ()):
            waiting[reader].discard(k)
            if not waiting[reader]:
                ready(reader)

    for k in tasks:
        if not waiting[k]:
            ready(k)
    pump()
    while arriving or computing:
        if arriving and (arriving[0][0] <= now or not computing):
            when, _, k = heapq.heappop(arriving)
            now = max(now, when) + 0.03
            if k[0] == "r":
                now += tasks[k][1] / ADD_RATE
            order.append(("arrive", k))
        else:
            k = heapq.heappop(computing)[2]
            now += tasks[k][1]
            order.append(("compute", k))
        finish(k)
        pump()
    return order, now


def make_kernel(sizes, unit, rows, experts_here, units):
    nz, nx, ny = sizes
    half_width = 3 * unit + LANES
    wide = unit + LANES
    reduce_widths = ((wide, unit, unit), (unit, wide, unit))
    gather_widths = ((wide, unit, wide), (unit, wide, wide))
    segments = (
        (((0, 0, wide),), ((0, wide, unit),), ((0, wide + unit, unit),)),
        (((0, 0, unit),), ((0, wide, unit), (unit, unit, LANES)), ((0, wide + unit, unit),)),
    )
    per_chunk = nz // HALVES
    spe = CAPACITY * nx * ny
    slots = experts_here * spe
    chunk_rows = per_chunk * spe
    group_tokens = nx * ny * rows
    exchange_bytes = experts_here * 2 * chunk_rows * units * 2
    tasks = build_tasks(sizes, gather_widths, reduce_widths, rows, exchange_bytes)
    order, _ = schedule(tasks)
    gathers = [k for k in tasks if k[0] == "g"]
    reduces = [k for k in tasks if k[0] == "r"]
    number = {k: n for n, k in enumerate(gathers)}
    number.update({k: n for n, k in enumerate(reduces)})
    buffers, buffer_of = {}, {}
    for k in reduces:
        p, c, stage = k[1:4]
        first = ORDERS[c][0]
        shape = []
        for a in sorted(ORDERS[c][:stage]):
            shape.append(sizes[a] // 2 if a == first else sizes[a])
        count = buffers.get((p, c, stage), (0,))[0]
        buffer_of[k] = count
        buffers[(p, c, stage)] = (count + 1,) + tuple(shape) + (rows, reduce_widths[p][c])
    buffer_keys = sorted(buffers)

    def kernel(
        x_ref, ids_ref, weight_ref, lane_ref, code_ref, code_t_ref, gate_hbm, up_hbm, down_hbm,
        out_ref, held01, held2, table_ref, gate_up, down, chosen, outs, pre_out, pre_in, fin_in,
        *rest,
    ):
        landing = dict(zip(buffer_keys, rest[: len(buffer_keys)]))
        (own_sem, pair_send, pair_recv, load_sem, load_send, load_recv,
         gather_send, gather_recv, reduce_send, reduce_recv,
         pre_send, pre_recv, fin_send, fin_recv) = rest[len(buffer_keys):]
        z = lax.axis_index("rep")
        e = lax.axis_index("exp")
        core = lax.rem(e, 2)
        chip = lax.div(e, 2)
        y = lax.rem(chip, ny)
        x = lax.div(chip, ny)
        here = (z, x, y)
        partner = (z, e + 1 - 2 * core)

        def held(p, c):
            return held2.at[p] if c == 2 else held01.at[c, p]

        def neighbour(axis, direction):
            moved = list(here)
            moved[axis] = lax.rem(here[axis] + direction + sizes[axis], sizes[axis])
            return (moved[0], (moved[1] * ny + moved[2]) * 2 + core)

        barrier = pltpu.get_barrier_semaphore()
        peers = [partner] + [neighbour(a, d) for a in range(3) for d in (1, -1)]
        for peer in peers:
            pl.semaphore_signal(barrier, inc=1, device_id=peer, device_id_type=MESH)

        experts = LANES // 2
        lane = lax.broadcasted_iota(jnp.int32, (rows, LANES), 1)
        named = jnp.zeros((rows, LANES), jnp.float32)
        weights = jnp.zeros((rows, LANES), jnp.float32)
        for k in range(ids_ref.shape[1]):
            name = ids_ref[:, k:k + 1]
            named = named + (lane == name).astype(jnp.float32)
            weights = weights + jnp.where(lane == name + experts, weight_ref[:, k:k + 1], 0.0)
        below = lax.broadcasted_iota(jnp.int32, (rows, rows), 0)
        across = lax.broadcasted_iota(jnp.int32, (rows, rows), 1)
        triangle = (across <= below).astype(jnp.bfloat16)
        rank = jnp.dot(triangle, named.astype(jnp.bfloat16), preferred_element_type=jnp.float32)
        table_ref[...] = (named * rank + weights).astype(jnp.bfloat16)

        pl.semaphore_wait(barrier, len(peers))

        def pieces(phase):
            mine = (z, x, y, pl.ds(0, rows))
            return (
                (0, unit, held01.at[(0, phase) + mine + (pl.ds(0, unit),)]),
                (unit, LANES, held01.at[(phase, phase) + mine + (pl.ds(unit, LANES),)]),
                (wide, unit, held01.at[(1, phase) + mine + (pl.ds(0, unit),)]),
                (wide + unit, unit, held2.at[(phase,) + mine + (pl.ds(0, unit),)]),
            )

        table_place = held2.at[core, z, x, y, pl.ds(0, rows), pl.ds(unit, LANES)]
        own_copies, pair_copies = [], []
        for n, (column, width, place) in enumerate(pieces(core)):
            start = pl.multiple_of(core * half_width + column, LANES)
            other = pl.multiple_of((1 - core) * half_width + column, LANES)
            own_copies.append((x_ref.at[:, pl.ds(start, width)], place))
            pair_copies.append((x_ref.at[:, pl.ds(other, width)], place))
        own_copies.append((table_ref, table_place))
        pair_copies.append((table_ref, table_place))
        own_copies = [
            pltpu.make_async_copy(a, b, own_sem.at[n]) for n, (a, b) in enumerate(own_copies)
        ]
        pair_copies = [
            pltpu.make_async_remote_copy(
                src_ref=a, dst_ref=b, send_sem=pair_send.at[n], recv_sem=pair_recv.at[n],
                device_id=partner, device_id_type=MESH,
            )
            for n, (a, b) in enumerate(pair_copies)
        ]
        for copy in pair_copies + own_copies:
            copy.start()

        local = experts_here // 2
        mine_experts = pl.ds(core * local, local)
        loads, sends = [], []
        for n, (source, target) in enumerate(
            (
                (gate_hbm, gate_up.at[mine_experts, 0]),
                (up_hbm, gate_up.at[mine_experts, 1]),
                (down_hbm, down.at[mine_experts]),
            )
        ):
            start = pl.multiple_of(core * half_width, LANES)
            other = pl.multiple_of((1 - core) * half_width, LANES)
            loads.append(
                pltpu.make_async_copy(
                    source.at[:, :, pl.ds(start, half_width)], target, load_sem.at[n]
                )
            )
            sends.append(
                pltpu.make_async_remote_copy(
                    src_ref=source.at[:, :, pl.ds(other, half_width)], dst_ref=target,
                    send_sem=load_send.at[n], recv_sem=load_recv.at[n], device_id=partner,
                    device_id_type=MESH,
                )
            )
        for copy in own_copies + pair_copies:
            copy.wait()
        for copy in loads + sends:
            copy.start()

        def block(p, c, stage, index, half, width):
            axes = ORDERS[c]
            where = []
            for a in range(3):
                if a == axes[stage]:
                    where.append(index)
                elif a in axes[:stage]:
                    if a == axes[0]:
                        where.append(pl.ds(half * (sizes[a] // 2), sizes[a] // 2))
                    else:
                        where.append(pl.ds(0, sizes[a]))
                else:
                    where.append(here[a])
            lead = (p,) if c == 2 else (c, p)
            ref = held2 if c == 2 else held01
            return ref.at[lead + tuple(where) + (pl.ds(0, rows), pl.ds(0, width))]

        def gather_copy(key, received):
            _, p, c, stage, d, s, h = key
            axis = ORDERS[c][stage]
            back = s if received else s - 1
            index = lax.rem(here[axis] - d * back + sizes[axis], sizes[axis])
            place = block(p, c, stage, index, h, gather_widths[p][c])
            n = number[key]
            return pltpu.make_async_remote_copy(
                src_ref=place, dst_ref=place, send_sem=gather_send.at[n],
                recv_sem=gather_recv.at[n], device_id=neighbour(axis, d), device_id_type=MESH,
            )

        def reduce_copy(key):
            _, p, c, stage, d, s, h = key
            axis = ORDERS[c][stage]
            size = sizes[axis]
            index = lax.rem(here[axis] + d * (size // 2 - s + 1) + size, size)
            n = number[key]
            return pltpu.make_async_remote_copy(
                src_ref=block(p, c, stage, index, h, reduce_widths[p][c]),
                dst_ref=landing[(p, c, stage)].at[buffer_of[key]],
                send_sem=reduce_send.at[n], recv_sem=reduce_recv.at[n],
                device_id=neighbour(axis, d), device_id_type=MESH,
            )

        def pre_copy(p, q):
            n = p * HALVES + q
            return pltpu.make_async_remote_copy(
                src_ref=pre_out.at[n], dst_ref=pre_in.at[n], send_sem=pre_send.at[n],
                recv_sem=pre_recv.at[n], device_id=partner, device_id_type=MESH,
            )

        def contract_last(a, b):
            return lax.dot_general(
                a, b, (((1,), (1,)), ((), ())), preferred_element_type=jnp.float32
            )

        base = chip * experts_here

        def group(p, c, gz, start, width):
            lead = (p,) if c == 2 else (c, p)
            ref = held2 if c == 2 else held01
            value = ref[lead + (gz, slice(None), slice(None), slice(None), pl.ds(start, width))]
            return value.reshape(group_tokens, width)

        def select(p, q, c):
            def one(g, carry):
                gz = q * per_chunk + g
                pick = (lane_ref[...] == base).astype(jnp.bfloat16)
                codes = contract_last(pick, group(p, 2, gz, unit, LANES))
                onehot = (codes == code_ref[...]).astype(jnp.bfloat16)
                for start, column, width in segments[p][c]:
                    picked = jnp.dot(
                        onehot, group(p, c, gz, start, width), preferred_element_type=jnp.float32
                    ).astype(jnp.bfloat16)
                    for n in range(experts_here):
                        chosen[n, pl.ds(pl.multiple_of(g * spe, 16), spe), pl.ds(column, width)] = (
                            picked[n * spe:(n + 1) * spe]
                        )
                return carry

            lax.fori_loop(0, per_chunk, one, 0)

        def project(p, q):
            def one(n, carry):
                for which in range(2):
                    pre_out[p * HALVES + q, n, which] = contract_last(
                        chosen[n], gate_up[n, which]
                    ).astype(jnp.bfloat16)
                return carry

            lax.fori_loop(0, experts_here, one, 0)

        def expand(p, q):
            index = p * HALVES + q

            def one(n, carry):
                values = []
                for which in range(2):
                    mine = pre_out[index, n, which].astype(jnp.float32)
                    values.append(mine + pre_in[index, n, which].astype(jnp.float32))
                hidden = values[0] / (1.0 + jnp.exp(-values[0])) * values[1]
                outcome = jnp.dot(
                    hidden.astype(jnp.bfloat16), down[n], preferred_element_type=jnp.float32
                ).astype(jnp.bfloat16)
                for g in range(per_chunk):
                    outs[g, pl.ds(pl.multiple_of(n * spe, 16), spe)] = (
                        outcome[g * spe:(g + 1) * spe]
                    )
                return carry

            lax.fori_loop(0, experts_here, one, 0)

        def combine(p, q):
            def one(g, carry):
                gz = q * per_chunk + g
                table = group(p, 2, gz, unit, LANES)
                pick = (lane_ref[...] == base).astype(jnp.bfloat16)
                weigh = (lane_ref[...] == base + experts).astype(jnp.bfloat16)
                codes = contract_last(table, pick)
                values = contract_last(table, weigh)
                scatter = jnp.where(codes == code_t_ref[...], values, 0.0).astype(jnp.bfloat16)
                for c in range(3):
                    lead = (p,) if c == 2 else (c, p)
                    ref = held2 if c == 2 else held01
                    for start, column, width in segments[p][c]:
                        summed = jnp.dot(
                            scatter, outs[g, :, pl.ds(column, width)],
                            preferred_element_type=jnp.float32,
                        )
                        where = lead + (gz, slice(None), slice(None), slice(None))
                        ref[where + (pl.ds(start, width),)] = summed.astype(jnp.bfloat16).reshape(
                            nx, ny, rows, width
                        )
                return carry

            lax.fori_loop(0, per_chunk, one, 0)

        def add_into(target, sources):
            lead = target.shape[:-2]

            def one_block(where):
                total = target[where].astype(jnp.float32)
                for source in sources:
                    total = total + source[where].astype(jnp.float32)
                target[where] = total.astype(jnp.bfloat16)

            if not lead:
                one_block(...)
                return

            def one(n, carry):
                if len(lead) == 1:
                    one_block((n,))
                else:
                    for m in range(lead[1]):
                        one_block((n, m))
                return carry

            lax.fori_loop(0, lead[0], one, 0)

        arrived = set()

        def reduce_arrival(key):
            reduce_copy(key).wait_recv()
            arrived.add(key)
            _, p, c, stage, d, s, h = key
            axis = ORDERS[c][stage]
            size = sizes[axis]
            last = size // 2
            width = reduce_widths[p][c]
            if s < last:
                index = lax.rem(here[axis] + d * (last - s) + size, size)
                add_into(
                    block(p, c, stage, index, h, width),
                    [landing[(p, c, stage)].at[buffer_of[key]]],
                )
                return
            parts = [k for k in reduces if k[:4] == key[:4] and k[5] == last and k[6] == h]
            if all(k in arrived for k in parts):
                add_into(
                    block(p, c, stage, here[axis], h, width),
                    [landing[(p, c, stage)].at[buffer_of[k]] for k in parts],
                )

        loaded = set()
        for kind, key in order:
            if kind == "start":
                if key[0] == "g":
                    gather_copy(key, False).start()
                elif key[0] == "r":
                    reduce_copy(key).start()
                else:
                    pre_copy(key[1], key[2]).start()
            elif kind == "arrive":
                if key[0] == "g":
                    gather_copy(key, True).wait_recv()
                elif key[0] == "r":
                    reduce_arrival(key)
                else:
                    pre_copy(key[1], key[2]).wait_recv()
            elif key[0] == "select":
                select(*key[1:])
            elif key[0] == "project":
                if not loaded:
                    loaded.add("all")
                    for copy in loads + sends:
                        copy.wait()
                project(*key[1:])
            elif key[0] == "expand":
                expand(*key[1:])
            else:
                if key[2] == 0:
                    for k in gathers:
                        if k[1] == key[1]:
                            gather_copy(k, False).wait_send()
                combine(*key[1:])

        last_copies = [
            pltpu.make_async_remote_copy(
                src_ref=place, dst_ref=fin_in.at[:, pl.ds(column, width)], send_sem=fin_send.at[n],
                recv_sem=fin_recv.at[n], device_id=partner, device_id_type=MESH,
            )
            for n, (column, width, place) in enumerate(pieces(1 - core))
        ]
        for copy in last_copies:
            copy.start()
        for column, width, place in pieces(core):
            start = pl.multiple_of(core * half_width + column, LANES)
            out_ref[:, pl.ds(start, width)] = place[...]
        for k in reduces:
            reduce_copy(k).wait_send()
        for p in range(PHASES):
            for q in range(HALVES):
                pre_copy(p, q).wait_send()
        for copy in last_copies:
            copy.wait()
        out_ref[:, pl.ds(pl.multiple_of((1 - core) * half_width, LANES), half_width)] = fin_in[...]

    bf16 = jnp.bfloat16
    dma = pltpu.SemaphoreType.DMA
    chunks = PHASES * HALVES
    pre_shape = (chunks, experts_here, 2, chunk_rows, units)
    scratch = [
        pltpu.VMEM((2, PHASES, nz, nx, ny, rows, wide), bf16),
        pltpu.VMEM((PHASES, nz, nx, ny, rows, wide), bf16),
        pltpu.VMEM((rows, LANES), bf16),
        pltpu.VMEM((experts_here, 2, units, half_width), bf16),
        pltpu.VMEM((experts_here, units, half_width), bf16),
        pltpu.VMEM((experts_here, chunk_rows, half_width), bf16),
        pltpu.VMEM((per_chunk, slots, half_width), bf16),
        pltpu.VMEM(pre_shape, bf16),
        pltpu.VMEM(pre_shape, bf16),
        pltpu.VMEM((rows, half_width), bf16),
        *[pltpu.VMEM(buffers[k], bf16) for k in buffer_keys],
        dma((5,)), dma((5,)), dma((5,)), dma((3,)), dma((3,)), dma((3,)),
        dma((len(gathers),)), dma((len(gathers),)), dma((len(reduces),)), dma((len(reduces),)),
        dma((chunks,)), dma((chunks,)), dma((4,)), dma((4,)),
    ]
    slot = np.arange(slots)
    token = np.arange(group_tokens)
    lane_constant = (np.arange(LANES)[None, :] - (slot // spe)[:, None]).astype(np.int32)
    same = (slot % spe // CAPACITY)[:, None] == (token // rows)[None, :]
    code = np.where(same, (slot % CAPACITY + 1)[:, None], -1).astype(np.float32)
    return kernel, scratch, (lane_constant, code, np.ascontiguousarray(code.T))


def solution(mesh):
    nz = mesh.shape["rep"]
    nx = int(round((mesh.shape["exp"] // 2) ** 0.5))
    ny = mesh.shape["exp"] // 2 // nx

    def on_device(tokens, routed_experts, route_weights, gate_weight, up_weight, down_weight):
        rows, width = tokens.shape
        local, units = gate_weight.shape[:2]
        unit = (width // 2 // LANES - 1) // 3 * LANES
        kernel, scratch, constants = make_kernel((nz, nx, ny), unit, rows, 2 * local, units)
        vmem = pl.BlockSpec(memory_space=pltpu.VMEM)
        hbm = pl.BlockSpec(memory_space=pl.ANY)
        return pl.pallas_call(
            kernel,
            out_shape=jax.ShapeDtypeStruct((rows, width), jnp.bfloat16),
            in_specs=[vmem] * 6 + [hbm] * 3,
            out_specs=vmem,
            scratch_shapes=scratch,
            compiler_params=pltpu.CompilerParams(
                collective_id=0, has_side_effects=True, vmem_limit_bytes=67_000_000
            ),
        )(tokens, routed_experts, route_weights, *constants, gate_weight, up_weight, down_weight)

    placed = (
        P(("rep", "exp"), None),
        P(("rep", "exp"), None),
        P(("rep", "exp"), None),
        P("exp", "rep", None),
        P("exp", "rep", None),
        P("exp", "rep", None),
    )
    return jax.shard_map(
        on_device, mesh=mesh, in_specs=placed, out_specs=P(("rep", "exp"), None), check_vma=False
    )
```

time: 559 us -> 189 us (0.34)
  waiting for transfers between devices: 320 us -> 0 us
  Pallas kernels: 0 us -> 185 us
  local copies, waits for them, and re-layouts: 93.1 us -> 4.27 us
  blocking collectives: 73.1 us -> 0 us
  matrix products: 29.5 us -> 0 us
  other arithmetic: 17.7 us -> 0 us
  between operations: 13.5 us -> 0.01 us
  starting transfers between devices: 7.92 us -> 0 us
    pallas_call x0 -> x1, Pallas kernels: none -> 185 us  [on_device(): pl.pallas_call(kernel, out_shape=jax.ShapeDtypeStruct((rows, width), jnp....]
    all_gather x1 -> x0, waiting for transfers between devices: 132 us -> none  [on_device(): rows_now = lax.all_gather(arrived, 'rep', axis=2, tiled=True)[0]]
    all_to_all x1 -> x0, waiting for transfers between devices: 130 us -> none  [on_device(): lax.all_to_all(outcomes, 'exp', split_axis=2, concat_axis=0, tiled=True)]
    reduce_scatter x1 -> x0, waiting for transfers between devices: 57.3 us -> none  [on_device(): summed = lax.psum_scatter(weighted, 'rep', scatter_dimension=0, tiled=True)]
    all_gather x2 -> x0, blocking collectives: 41.9 us -> none  [the longest x1 21.1 us: routing_column(): lax.all_gather(as_float, 'rep', axis=0, tiled=True)]
    gather x1 -> x0, local copies, waits for them, and re-layouts: 34.6 us -> none  [on_device(): returned[expert_index, replica_index, place_index].astype(jnp.float32)]
    all_to_all x1 -> x0, blocking collectives: 31.2 us -> none  [on_device(): lax.all_to_all(buffer, 'exp', split_axis=0, concat_axis=2, tiled=True)]
    dot_general x3 -> x0, matrix products: 29.5 us -> none  [the longest x1 15.9 us: on_device(): jnp.einsum('emf,efd->emd', hidden, down_weight, preferred_element_type=jn...]
  transfers between devices with their start and end apart: 3 -> 0, of which waited for: 3 -> 0; matrix products, arithmetic and copies ran while one was open for 1% -> 0% of each run, Pallas kernels for 0% -> 0%
where the time goes in v2:
time: 189 us
  Pallas kernels  185 us (98%)
  local copies, waits for them, and re-layouts  4.27 us (2%)
    pallas_call x1, Pallas kernels, on_device(): pl.pallas_call(kernel, out_shape=jax.ShapeDtypeStruct((rows, width), jnp....  185 us
    unnamed x3, local copies, waits for them, and re-layouts  4.27 us

profile of v2, /device:TPU:1, one launch (start us, length us, event | category | flops | bytes accessed | tf_op | source)
XLA Modules:
  0.0 189.2 jit_solution(7135509304906045091)
XLA Ops:
  0.0 1.4 copy.10.ids_ref
  1.4 1.4 copy.11.weight_ref
  2.7 184.9 %shard_map.91 = bf16[16,4096]{1,0:T(8,128)(2,1)} custom-call(bf16[16,4096]{1,0:T(8,128)(2,1)} %x_ref.1, s32[16,8]{1,0:T(8,128)} %copy.10.ids_ref, f32[16,8]{1,0:T(8,128)} %copy.11.weight_ref, s32[192,128]{1,0:T(8,128)} %constant.6.clone.lane_ref, f32[192,256]{1,0:T(8,128)} %constant.7.clone.code_ref, f32[256,192]{1,0:T(8,128)} %constant.8.clone.code_t_ref, ...), custom_call_target="tpu_custom_call" | custom-call | tf_op jit(solution)/shard_map/pallas_call | solution.py:587
  187.6 1.6 copy.13

commit v3 on v2

--- a/solution.py
+++ b/solution.py
@@ -18,7 +18,7 @@
 RATE = 46000.0
 PAIR_RATE = 150000.0
 LATENCY = 1.8
-LOOK = 4.0
+LOOK = 2.0
 ADD_RATE = 1.5e6
 COSTS = {"select": 0.85, "project": 2.5, "expand": 1.9, "combine": 1.9}
 
@@ -202,12 +202,13 @@
     buffer_keys = sorted(buffers)
 
     def kernel(
-        x_ref, ids_ref, weight_ref, lane_ref, code_ref, code_t_ref, gate_hbm, up_hbm, down_hbm,
-        out_ref, held01, held2, table_ref, gate_up, down, chosen, outs, pre_out, pre_in, fin_in,
+        ids_ref, weight_ref, x_ref, lane_hbm, code_hbm, code_t_hbm, gate_hbm, up_hbm, down_hbm,
+        out_ref, held01, held2, table_ref, lane_ref, code_ref, code_t_ref, gate_up, down, chosen,
+        outs, pre_out, pre_in, fin_in,
         *rest,
     ):
         landing = dict(zip(buffer_keys, rest[: len(buffer_keys)]))
-        (own_sem, pair_send, pair_recv, load_sem, load_send, load_recv,
+        (constant_sem, own_sem, pair_send, pair_recv, load_sem, load_send, load_recv,
          gather_send, gather_recv, reduce_send, reduce_recv,
          pre_send, pre_recv, fin_send, fin_recv) = rest[len(buffer_keys):]
         z = lax.axis_index("rep")
@@ -227,21 +228,40 @@
             moved[axis] = lax.rem(here[axis] + direction + sizes[axis], sizes[axis])
             return (moved[0], (moved[1] * ny + moved[2]) * 2 + core)
 
+        def contract_last(a, b):
+            return lax.dot_general(
+                a, b, (((1,), (1,)), ((), ())), preferred_element_type=jnp.float32
+            )
+
         barrier = pltpu.get_barrier_semaphore()
         peers = [partner] + [neighbour(a, d) for a in range(3) for d in (1, -1)]
         for peer in peers:
             pl.semaphore_signal(barrier, inc=1, device_id=peer, device_id_type=MESH)
 
+        constants = [
+            pltpu.make_async_copy(a, b, constant_sem.at[n])
+            for n, (a, b) in enumerate(
+                ((lane_hbm, lane_ref), (code_hbm, code_ref), (code_t_hbm, code_t_ref))
+            )
+        ]
+        for copy in constants:
+            copy.start()
+
         experts = LANES // 2
         lane = lax.broadcasted_iota(jnp.int32, (rows, LANES), 1)
         named = jnp.zeros((rows, LANES), jnp.float32)
         weights = jnp.zeros((rows, LANES), jnp.float32)
-        for k in range(ids_ref.shape[1]):
-            name = ids_ref[:, k:k + 1]
-            named = named + (lane == name).astype(jnp.float32)
-            weights = weights + jnp.where(lane == name + experts, weight_ref[:, k:k + 1], 0.0)
         below = lax.broadcasted_iota(jnp.int32, (rows, rows), 0)
         across = lax.broadcasted_iota(jnp.int32, (rows, rows), 1)
+        same = (across == below).astype(jnp.float32).astype(jnp.bfloat16)
+        flipped = [
+            contract_last(same, ref[...].astype(jnp.float32).astype(jnp.bfloat16))
+            for ref in (ids_ref, weight_ref)
+        ]
+        for k in range(ids_ref.shape[0]):
+            name = flipped[0][:, k:k + 1].astype(jnp.int32)
+            named = named + (lane == name).astype(jnp.float32)
+            weights = weights + jnp.where(lane == name + experts, flipped[1][:, k:k + 1], 0.0)
         triangle = (across <= below).astype(jnp.bfloat16)
         rank = jnp.dot(triangle, named.astype(jnp.bfloat16), preferred_element_type=jnp.float32)
         table_ref[...] = (named * rank + weights).astype(jnp.bfloat16)
@@ -355,11 +375,6 @@
             return pltpu.make_async_remote_copy(
                 src_ref=pre_out.at[n], dst_ref=pre_in.at[n], send_sem=pre_send.at[n],
                 recv_sem=pre_recv.at[n], device_id=partner, device_id_type=MESH,
-            )
-
-        def contract_last(a, b):
-            return lax.dot_general(
-                a, b, (((1,), (1,)), ((), ())), preferred_element_type=jnp.float32
             )
 
         base = chip * experts_here
@@ -507,10 +522,14 @@
                 else:
                     pre_copy(key[1], key[2]).wait_recv()
             elif key[0] == "select":
+                if "constants" not in loaded:
+                    loaded.add("constants")
+                    for copy in constants:
+                        copy.wait()
                 select(*key[1:])
             elif key[0] == "project":
-                if not loaded:
-                    loaded.add("all")
+                if "weights" not in loaded:
+                    loaded.add("weights")
                     for copy in loads + sends:
                         copy.wait()
                 project(*key[1:])
@@ -552,6 +571,9 @@
         pltpu.VMEM((2, PHASES, nz, nx, ny, rows, wide), bf16),
         pltpu.VMEM((PHASES, nz, nx, ny, rows, wide), bf16),
         pltpu.VMEM((rows, LANES), bf16),
+        pltpu.VMEM((slots, LANES), jnp.int32),
+        pltpu.VMEM((slots, group_tokens), jnp.float32),
+        pltpu.VMEM((group_tokens, slots), jnp.float32),
         pltpu.VMEM((experts_here, 2, units, half_width), bf16),
         pltpu.VMEM((experts_here, units, half_width), bf16),
         pltpu.VMEM((experts_here, chunk_rows, half_width), bf16),
@@ -560,7 +582,7 @@
         pltpu.VMEM(pre_shape, bf16),
         pltpu.VMEM((rows, half_width), bf16),
         *[pltpu.VMEM(buffers[k], bf16) for k in buffer_keys],
-        dma((5,)), dma((5,)), dma((5,)), dma((3,)), dma((3,)), dma((3,)),
+        dma((3,)), dma((5,)), dma((5,)), dma((5,)), dma((3,)), dma((3,)), dma((3,)),
         dma((len(gathers),)), dma((len(gathers),)), dma((len(reduces),)), dma((len(reduces),)),
         dma((chunks,)), dma((chunks,)), dma((4,)), dma((4,)),
     ]
@@ -587,13 +609,16 @@
         return pl.pallas_call(
             kernel,
             out_shape=jax.ShapeDtypeStruct((rows, width), jnp.bfloat16),
-            in_specs=[vmem] * 6 + [hbm] * 3,
+            in_specs=[vmem] * 2 + [hbm] * 7,
             out_specs=vmem,
             scratch_shapes=scratch,
             compiler_params=pltpu.CompilerParams(
                 collective_id=0, has_side_effects=True, vmem_limit_bytes=67_000_000
             ),
-        )(tokens, routed_experts, route_weights, *constants, gate_weight, up_weight, down_weight)
+        )(
+            routed_experts.T, route_weights.T, tokens, *constants, gate_weight, up_weight,
+            down_weight,
+        )
 
     placed = (
         P(("rep", "exp"), None),

time: 189 us -> 183 us (0.968)
  Pallas kernels: 185 us -> 181 us
  local copies, waits for them, and re-layouts: 4.27 us -> 1.57 us
    pallas_call x1, Pallas kernels: 185 us -> 181 us  [on_device(): pl.pallas_call(kernel, out_shape=jax.ShapeDtypeStruct((rows, width), jnp....]
    unnamed x3 -> x1, local copies, waits for them, and re-layouts: 4.27 us -> 1.57 us
where the time goes in v3:
time: 183 us
  Pallas kernels  181 us (99%)
    pallas_call x1, Pallas kernels, on_device(): pl.pallas_call(kernel, out_shape=jax.ShapeDtypeStruct((rows, width), jnp....  181 us

profile of v3, /device:TPU:1, one launch (start us, length us, event | category | flops | bytes accessed | tf_op | source)
XLA Modules:
  0.0 182.6 jit_solution(1269677752384790055)
XLA Ops:
  0.0 181.0 %shard_map.91 = bf16[16,4096]{1,0:T(8,128)(2,1)} custom-call(s32[8,16]{1,0:T(8,128)} %bitcast.2, f32[8,16]{1,0:T(8,128)} %bitcast.3, bf16[16,4096]{1,0:T(8,128)(2,1)} %x_ref.1, s32[192,128]{1,0:T(8,128)} %constant.6.clone.lane_hbm, f32[192,256]{1,0:T(8,128)} %constant.7.clone.code_hbm, f32[256,192]{1,0:T(8,128)} %constant.8.clone.code_t_hbm, ...), custom_call_target="tpu_custom_call" | custom-call | tf_op jit(solution)/shard_map/pallas_call | solution.py:609
  181.0 1.6 copy.11

commit v4 on v3

--- a/solution.py
+++ b/solution.py
@@ -20,7 +20,7 @@
 LATENCY = 1.8
 LOOK = 2.0
 ADD_RATE = 1.5e6
-COSTS = {"select": 0.85, "project": 2.5, "expand": 1.9, "combine": 1.9}
+COSTS = {"select": 0.8, "fetch": 0.3, "pick": 0.3, "project": 2.5, "expand": 1.9, "combine": 1.2, "spread": 0.3}
 
 
 def steps_of(size, split, long, gathering):
@@ -40,14 +40,16 @@
     return found
 
 
-def block_bytes(sizes, width, rows, order, stage):
+def block_bytes(sizes, width, rows, order, stage, slots):
     total = rows * width * 2
+    if order[2] == 0 and stage == 2:
+        return slots * width
     for axis in order[:stage]:
         total *= sizes[axis]
     return total // 2 if stage else total
 
 
-def build_tasks(sizes, gather_widths, reduce_widths, rows, exchange_bytes):
+def build_tasks(sizes, gather_widths, reduce_widths, rows, exchange_bytes, slots):
     tasks = {}
     chunk_before = None
     for p in range(PHASES):
@@ -60,23 +62,36 @@
                         needs = {("g", p, c, stage, d, s - 1, h)}
                     elif stage == 0:
                         needs = set()
+                    elif c == 2 and stage == 2:
+                        needs = {("pick", p)}
                     else:
                         needs = {
                             k for k in tasks
                             if k[:4] == ("g", p, c, stage - 1) and (stage == 1 or k[6] == h)
                         }
                     key = ("g", p, c, stage, d, s, h)
-                    size = block_bytes(sizes, gather_widths[p][c], rows, order, stage)
+                    width = reduce_widths[c] if stage == 2 else gather_widths[c]
+                    size = block_bytes(sizes, width, rows, order, stage, slots)
                     tasks[key] = ((axis, d), size, needs)
+                if c == 2 and stage == 1:
+                    plane = {k for k in tasks if k[:4] == ("g", p, 2, 1)}
+                    tasks[("pick", p)] = (None, COSTS["pick"], plane)
+                    size = sizes[1] * sizes[2] * rows * LANES * 2
+                    for d, s, h in steps_of(sizes[0], False, -1, True):
+                        needs = {("t", p, 3, 2, d, s - 1, h)} if s > 1 else {("pick", p)}
+                        tasks[("t", p, 3, 2, d, s, h)] = ((0, d), size, needs)
+                    arrivals[3] = {k for k in tasks if k[:2] == ("t", p)}
             arrivals[c] = {k for k in tasks if k[:4] == ("g", p, c, 2)}
         for q in range(HALVES):
             for c in range(3):
-                needs = set(arrivals[2])
                 if c < 2:
-                    needs |= {k for k in arrivals[c] if k[6] == q}
+                    needs = arrivals[3] | {k for k in arrivals[c] if k[6] == q}
+                else:
+                    needs = set(arrivals[2])
                 if chunk_before is not None:
                     needs.add(("project",) + chunk_before)
-                tasks[("select", p, q, c)] = (None, COSTS["select"], needs)
+                cost = COSTS["select"] if c < 2 else COSTS["fetch"]
+                tasks[("select", p, q, c)] = (None, cost, needs)
             tasks[("project", p, q)] = (
                 None, COSTS["project"], {("select", p, q, c) for c in range(3)}
             )
@@ -87,6 +102,7 @@
             tasks[("expand", p, q)] = (None, COSTS["expand"], needs)
             tasks[("combine", p, q)] = (None, COSTS["combine"], {("expand", p, q)})
             chunk_before = (p, q)
+        tasks[("spread", p)] = (None, COSTS["spread"], set())
         for c, order in enumerate(ORDERS):
             for stage in (2, 1, 0):
                 axis = order[stage]
@@ -94,8 +110,12 @@
                 for d, s, h in steps:
                     if (d, s - 1, h) in steps:
                         needs = {("r", p, c, stage, d, s - 1, h)}
+                    elif stage == 2 and c == 2:
+                        needs = {("expand", p, q) for q in range(HALVES)}
                     elif stage == 2:
-                        needs = {("combine", p, q) for q in range(HALVES) if c == 2 or q == h}
+                        needs = {("combine", p, h)}
+                    elif stage == 1 and c == 2:
+                        needs = {("spread", p)}
                     else:
                         needs = {
                             k for k in tasks
@@ -104,17 +124,20 @@
                             and (stage == 0 or k[6] == h)
                         }
                     key = ("r", p, c, stage, d, s, h)
-                    size = block_bytes(sizes, reduce_widths[p][c], rows, order, stage)
+                    size = block_bytes(sizes, reduce_widths[c], rows, order, stage, slots)
                     tasks[key] = ((axis, d), size, needs)
+                    if c == 2 and stage == 2 and s == sizes[0] // 2:
+                        tasks[("spread", p)][2].add(key)
     return tasks
 
 
 def priority(key):
-    if key[0] == "g":
+    if key[0] in "gt":
         return key[1] * 10 + key[3]
     if key[0] == "r":
         return 20 + key[1] * 10 + key[3]
-    return key[1] + {"select": 40, "project": 40, "x": 0, "expand": 10, "combine": 10}[key[0]]
+    first = {"pick": -10, "spread": -10, "x": 0, "expand": 10, "combine": 10}
+    return key[1] + first.get(key[0], 40)
 
 
 def schedule(tasks):
@@ -167,25 +190,20 @@
     return order, now
 
 
-def make_kernel(sizes, unit, rows, experts_here, units):
+def make_kernel(sizes, widths, rows, experts_here, units):
     nz, nx, ny = sizes
-    half_width = 3 * unit + LANES
-    wide = unit + LANES
-    reduce_widths = ((wide, unit, unit), (unit, wide, unit))
-    gather_widths = ((wide, unit, wide), (unit, wide, wide))
-    segments = (
-        (((0, 0, wide),), ((0, wide, unit),), ((0, wide + unit, unit),)),
-        (((0, 0, unit),), ((0, wide, unit), (unit, unit, LANES)), ((0, wide + unit, unit),)),
-    )
+    half_width = sum(widths)
+    offsets = (0, widths[0], widths[0] + widths[1])
+    gather_widths = (widths[0], widths[1], widths[2] + LANES)
     per_chunk = nz // HALVES
     spe = CAPACITY * nx * ny
     slots = experts_here * spe
     chunk_rows = per_chunk * spe
     group_tokens = nx * ny * rows
     exchange_bytes = experts_here * 2 * chunk_rows * units * 2
-    tasks = build_tasks(sizes, gather_widths, reduce_widths, rows, exchange_bytes)
+    tasks = build_tasks(sizes, gather_widths, widths, rows, exchange_bytes, slots)
     order, _ = schedule(tasks)
-    gathers = [k for k in tasks if k[0] == "g"]
+    gathers = [k for k in tasks if k[0] in "gt"]
     reduces = [k for k in tasks if k[0] == "r"]
     number = {k: n for n, k in enumerate(gathers)}
     number.update({k: n for n, k in enumerate(reduces)})
@@ -198,12 +216,15 @@
             shape.append(sizes[a] // 2 if a == first else sizes[a])
         count = buffers.get((p, c, stage), (0,))[0]
         buffer_of[k] = count
-        buffers[(p, c, stage)] = (count + 1,) + tuple(shape) + (rows, reduce_widths[p][c])
+        if c == 2 and stage == 2:
+            buffers[(p, c, stage)] = (count + 1, slots // 2, widths[c])
+        else:
+            buffers[(p, c, stage)] = (count + 1,) + tuple(shape) + (rows, widths[c])
     buffer_keys = sorted(buffers)
 
     def kernel(
         ids_ref, weight_ref, x_ref, lane_hbm, code_hbm, code_t_hbm, gate_hbm, up_hbm, down_hbm,
-        out_ref, held01, held2, table_ref, lane_ref, code_ref, code_t_ref, gate_up, down, chosen,
+        out_ref, held01, plane, slotted, tables, table_ref, lane_ref, code_ref, code_t_ref, gate_up, down, chosen,
         outs, pre_out, pre_in, fin_in,
         *rest,
     ):
@@ -219,9 +240,6 @@
         x = lax.div(chip, ny)
         here = (z, x, y)
         partner = (z, e + 1 - 2 * core)
-
-        def held(p, c):
-            return held2.at[p] if c == 2 else held01.at[c, p]
 
         def neighbour(axis, direction):
             moved = list(here)
@@ -271,13 +289,12 @@
         def pieces(phase):
             mine = (z, x, y, pl.ds(0, rows))
             return (
-                (0, unit, held01.at[(0, phase) + mine + (pl.ds(0, unit),)]),
-                (unit, LANES, held01.at[(phase, phase) + mine + (pl.ds(unit, LANES),)]),
-                (wide, unit, held01.at[(1, phase) + mine + (pl.ds(0, unit),)]),
-                (wide + unit, unit, held2.at[(phase,) + mine + (pl.ds(0, unit),)]),
-            )
-
-        table_place = held2.at[core, z, x, y, pl.ds(0, rows), pl.ds(unit, LANES)]
+                (offsets[0], widths[0], held01.at[(0, phase) + mine + (pl.ds(0, widths[0]),)]),
+                (offsets[1], widths[1], held01.at[(1, phase) + mine + (pl.ds(0, widths[1]),)]),
+                (offsets[2], widths[2], plane.at[phase, x, y, pl.ds(0, rows), pl.ds(0, widths[2])]),
+            )
+
+        table_place = plane.at[core, x, y, pl.ds(0, rows), pl.ds(widths[2], LANES)]
         own_copies, pair_copies = [], []
         for n, (column, width, place) in enumerate(pieces(core)):
             start = pl.multiple_of(core * half_width + column, LANES)
@@ -329,6 +346,11 @@
             copy.start()
 
         def block(p, c, stage, index, half, width):
+            if c == 3:
+                return tables.at[p, index]
+            if c == 2 and stage == 2:
+                part = slots // 2
+                return slotted.at[p, index, pl.ds(half * part, part)]
             axes = ORDERS[c]
             where = []
             for a in range(3):
@@ -341,16 +363,16 @@
                         where.append(pl.ds(0, sizes[a]))
                 else:
                     where.append(here[a])
-            lead = (p,) if c == 2 else (c, p)
-            ref = held2 if c == 2 else held01
-            return ref.at[lead + tuple(where) + (pl.ds(0, rows), pl.ds(0, width))]
+            if c == 2:
+                return plane.at[(p,) + tuple(where[1:]) + (pl.ds(0, rows), pl.ds(0, width))]
+            return held01.at[(c, p) + tuple(where) + (pl.ds(0, rows), pl.ds(0, width))]
 
         def gather_copy(key, received):
             _, p, c, stage, d, s, h = key
-            axis = ORDERS[c][stage]
+            axis = ORDERS[c][stage] if c < 3 else 0
             back = s if received else s - 1
             index = lax.rem(here[axis] - d * back + sizes[axis], sizes[axis])
-            place = block(p, c, stage, index, h, gather_widths[p][c])
+            place = block(p, c, stage, index, h, gather_widths[c] if c < 3 else LANES)
             n = number[key]
             return pltpu.make_async_remote_copy(
                 src_ref=place, dst_ref=place, send_sem=gather_send.at[n],
@@ -364,7 +386,7 @@
             index = lax.rem(here[axis] + d * (size // 2 - s + 1) + size, size)
             n = number[key]
             return pltpu.make_async_remote_copy(
-                src_ref=block(p, c, stage, index, h, reduce_widths[p][c]),
+                src_ref=block(p, c, stage, index, h, widths[c]),
                 dst_ref=landing[(p, c, stage)].at[buffer_of[key]],
                 send_sem=reduce_send.at[n], recv_sem=reduce_recv.at[n],
                 device_id=neighbour(axis, d), device_id_type=MESH,
@@ -379,26 +401,48 @@
 
         base = chip * experts_here
 
-        def group(p, c, gz, start, width):
-            lead = (p,) if c == 2 else (c, p)
-            ref = held2 if c == 2 else held01
-            value = ref[lead + (gz, slice(None), slice(None), slice(None), pl.ds(start, width))]
-            return value.reshape(group_tokens, width)
+        def table_of(p, gz):
+            return tables[p, gz].reshape(group_tokens, LANES)
+
+        def onehot_of(table):
+            wanted = (lane_ref[...] == base).astype(jnp.bfloat16)
+            return (contract_last(wanted, table) == code_ref[...]).astype(jnp.bfloat16)
+
+        def scatter_of(table):
+            wanted = (lane_ref[...] == base).astype(jnp.bfloat16)
+            weigh = (lane_ref[...] == base + experts).astype(jnp.bfloat16)
+            codes = contract_last(table, wanted)
+            values = contract_last(table, weigh)
+            return jnp.where(codes == code_t_ref[...], values, 0.0).astype(jnp.bfloat16)
+
+        def pick_rows(p):
+            tables[p, z] = plane[p, :, :, :, pl.ds(widths[2], LANES)]
+            value = plane[p, :, :, :, pl.ds(0, widths[2])].reshape(group_tokens, widths[2])
+            slotted[p, z] = jnp.dot(
+                onehot_of(table_of(p, z)), value, preferred_element_type=jnp.float32
+            ).astype(jnp.bfloat16)
+
+        def spread(p):
+            plane[p, :, :, :, pl.ds(0, widths[2])] = jnp.dot(
+                scatter_of(table_of(p, z)), slotted[p, z], preferred_element_type=jnp.float32
+            ).astype(jnp.bfloat16).reshape(nx, ny, rows, widths[2])
 
         def select(p, q, c):
+            columns = pl.ds(offsets[c], widths[c])
+
             def one(g, carry):
                 gz = q * per_chunk + g
-                pick = (lane_ref[...] == base).astype(jnp.bfloat16)
-                codes = contract_last(pick, group(p, 2, gz, unit, LANES))
-                onehot = (codes == code_ref[...]).astype(jnp.bfloat16)
-                for start, column, width in segments[p][c]:
+                if c == 2:
+                    picked = slotted[p, gz]
+                else:
+                    value = held01[c, p, gz].reshape(group_tokens, widths[c])
                     picked = jnp.dot(
-                        onehot, group(p, c, gz, start, width), preferred_element_type=jnp.float32
+                        onehot_of(table_of(p, gz)), value, preferred_element_type=jnp.float32
                     ).astype(jnp.bfloat16)
-                    for n in range(experts_here):
-                        chosen[n, pl.ds(pl.multiple_of(g * spe, 16), spe), pl.ds(column, width)] = (
-                            picked[n * spe:(n + 1) * spe]
-                        )
+                for n in range(experts_here):
+                    chosen[n, pl.ds(pl.multiple_of(g * spe, 16), spe), columns] = (
+                        picked[n * spe:(n + 1) * spe]
+                    )
                 return carry
 
             lax.fori_loop(0, per_chunk, one, 0)
@@ -426,9 +470,10 @@
                     hidden.astype(jnp.bfloat16), down[n], preferred_element_type=jnp.float32
                 ).astype(jnp.bfloat16)
                 for g in range(per_chunk):
-                    outs[g, pl.ds(pl.multiple_of(n * spe, 16), spe)] = (
-                        outcome[g * spe:(g + 1) * spe]
-                    )
+                    place = pl.ds(pl.multiple_of(n * spe, 16), spe)
+                    part = outcome[g * spe:(g + 1) * spe]
+                    outs[g, place] = part[:, :offsets[2]]
+                    slotted[p, q * per_chunk + g, place] = part[:, offsets[2]:]
                 return carry
 
             lax.fori_loop(0, experts_here, one, 0)
@@ -436,24 +481,12 @@
         def combine(p, q):
             def one(g, carry):
                 gz = q * per_chunk + g
-                table = group(p, 2, gz, unit, LANES)
-                pick = (lane_ref[...] == base).astype(jnp.bfloat16)
-                weigh = (lane_ref[...] == base + experts).astype(jnp.bfloat16)
-                codes = contract_last(table, pick)
-                values = contract_last(table, weigh)
-                scatter = jnp.where(codes == code_t_ref[...], values, 0.0).astype(jnp.bfloat16)
-                for c in range(3):
-                    lead = (p,) if c == 2 else (c, p)
-                    ref = held2 if c == 2 else held01
-                    for start, column, width in segments[p][c]:
-                        summed = jnp.dot(
-                            scatter, outs[g, :, pl.ds(column, width)],
-                            preferred_element_type=jnp.float32,
-                        )
-                        where = lead + (gz, slice(None), slice(None), slice(None))
-                        ref[where + (pl.ds(start, width),)] = summed.astype(jnp.bfloat16).reshape(
-                            nx, ny, rows, width
-                        )
+                scatter = scatter_of(table_of(p, gz))
+                for c in range(2):
+                    held01[c, p, gz] = jnp.dot(
+                        scatter, outs[g, :, pl.ds(offsets[c], widths[c])],
+                        preferred_element_type=jnp.float32,
+                    ).astype(jnp.bfloat16).reshape(nx, ny, rows, widths[c])
                 return carry
 
             lax.fori_loop(0, per_chunk, one, 0)
@@ -490,7 +523,7 @@
             axis = ORDERS[c][stage]
             size = sizes[axis]
             last = size // 2
-            width = reduce_widths[p][c]
+            width = widths[c]
             if s < last:
                 index = lax.rem(here[axis] + d * (last - s) + size, size)
                 add_into(
@@ -508,24 +541,28 @@
         loaded = set()
         for kind, key in order:
             if kind == "start":
-                if key[0] == "g":
+                if key[0] in "gt":
                     gather_copy(key, False).start()
                 elif key[0] == "r":
                     reduce_copy(key).start()
                 else:
                     pre_copy(key[1], key[2]).start()
             elif kind == "arrive":
-                if key[0] == "g":
+                if key[0] in "gt":
                     gather_copy(key, True).wait_recv()
                 elif key[0] == "r":
                     reduce_arrival(key)
                 else:
                     pre_copy(key[1], key[2]).wait_recv()
-            elif key[0] == "select":
+            elif key[0] == "pick":
                 if "constants" not in loaded:
                     loaded.add("constants")
                     for copy in constants:
                         copy.wait()
+                pick_rows(key[1])
+            elif key[0] == "spread":
+                spread(key[1])
+            elif key[0] == "select":
                 select(*key[1:])
             elif key[0] == "project":
                 if "weights" not in loaded:
@@ -534,12 +571,12 @@
                         copy.wait()
                 project(*key[1:])
             elif key[0] == "expand":
-                expand(*key[1:])
-            else:
                 if key[2] == 0:
                     for k in gathers:
                         if k[1] == key[1]:
                             gather_copy(k, False).wait_send()
+                expand(*key[1:])
+            else:
                 combine(*key[1:])
 
         last_copies = [
@@ -568,8 +605,10 @@
     chunks = PHASES * HALVES
     pre_shape = (chunks, experts_here, 2, chunk_rows, units)
     scratch = [
-        pltpu.VMEM((2, PHASES, nz, nx, ny, rows, wide), bf16),
-        pltpu.VMEM((PHASES, nz, nx, ny, rows, wide), bf16),
+        pltpu.VMEM((2, PHASES, nz, nx, ny, rows, widths[0]), bf16),
+        pltpu.VMEM((PHASES, nx, ny, rows, widths[2] + LANES), bf16),
+        pltpu.VMEM((PHASES, nz, slots, widths[2]), bf16),
+        pltpu.VMEM((PHASES, nz, nx, ny, rows, LANES), bf16),
         pltpu.VMEM((rows, LANES), bf16),
         pltpu.VMEM((slots, LANES), jnp.int32),
         pltpu.VMEM((slots, group_tokens), jnp.float32),
@@ -577,14 +616,14 @@
         pltpu.VMEM((experts_here, 2, units, half_width), bf16),
         pltpu.VMEM((experts_here, units, half_width), bf16),
         pltpu.VMEM((experts_here, chunk_rows, half_width), bf16),
-        pltpu.VMEM((per_chunk, slots, half_width), bf16),
+        pltpu.VMEM((per_chunk, slots, offsets[2]), bf16),
         pltpu.VMEM(pre_shape, bf16),
         pltpu.VMEM(pre_shape, bf16),
         pltpu.VMEM((rows, half_width), bf16),
         *[pltpu.VMEM(buffers[k], bf16) for k in buffer_keys],
-        dma((3,)), dma((5,)), dma((5,)), dma((5,)), dma((3,)), dma((3,)), dma((3,)),
+        dma((3,)), dma((4,)), dma((4,)), dma((4,)), dma((3,)), dma((3,)), dma((3,)),
         dma((len(gathers),)), dma((len(gathers),)), dma((len(reduces),)), dma((len(reduces),)),
-        dma((chunks,)), dma((chunks,)), dma((4,)), dma((4,)),
+        dma((chunks,)), dma((chunks,)), dma((3,)), dma((3,)),
     ]
     slot = np.arange(slots)
     token = np.arange(group_tokens)
@@ -602,8 +641,9 @@
     def on_device(tokens, routed_experts, route_weights, gate_weight, up_weight, down_weight):
         rows, width = tokens.shape
         local, units = gate_weight.shape[:2]
-        unit = (width // 2 // LANES - 1) // 3 * LANES
-        kernel, scratch, constants = make_kernel((nz, nx, ny), unit, rows, 2 * local, units)
+        thin = max(1, 5 * (width // 2 // LANES) // 16) * LANES
+        widths = (thin, thin, width // 2 - 2 * thin)
+        kernel, scratch, constants = make_kernel((nz, nx, ny), widths, rows, 2 * local, units)
         vmem = pl.BlockSpec(memory_space=pltpu.VMEM)
         hbm = pl.BlockSpec(memory_space=pl.ANY)
         return pl.pallas_call(

time: 183 us -> 170 us (0.929)
  Pallas kernels: 181 us -> 168 us
    pallas_call x1, Pallas kernels: 181 us -> 168 us  [on_device(): pl.pallas_call(kernel, out_shape=jax.ShapeDtypeStruct((rows, width), jnp....]
where the time goes in v4:
time: 170 us
  Pallas kernels  168 us (99%)
    pallas_call x1, Pallas kernels, on_device(): pl.pallas_call(kernel, out_shape=jax.ShapeDtypeStruct((rows, width), jnp....  168 us

profile of v4, /device:TPU:1, one launch (start us, length us, event | category | flops | bytes accessed | tf_op | source)
XLA Modules:
  0.0 169.7 jit_solution(18244811211292339817)
XLA Ops:
  0.0 168.2 %shard_map.91 = bf16[16,4096]{1,0:T(8,128)(2,1)} custom-call(s32[8,16]{1,0:T(8,128)} %bitcast.2, f32[8,16]{1,0:T(8,128)} %bitcast.3, bf16[16,4096]{1,0:T(8,128)(2,1)} %x_ref.1, s32[192,128]{1,0:T(8,128)} %constant.6.clone.lane_hbm, f32[192,256]{1,0:T(8,128)} %constant.7.clone.code_hbm, f32[256,192]{1,0:T(8,128)} %constant.8.clone.code_t_hbm, ...), custom_call_target="tpu_custom_call" | custom-call | tf_op jit(solution)/shard_map/pallas_call | solution.py:649
  168.2 1.6 copy.11

commit v5 on v4

--- a/solution.py
+++ b/solution.py
@@ -17,7 +17,7 @@
 LONG = (1, -1, 1)
 RATE = 46000.0
 PAIR_RATE = 150000.0
-LATENCY = 1.8
+LATENCY = 3.0
 LOOK = 2.0
 ADD_RATE = 1.5e6
 COSTS = {"select": 0.8, "fetch": 0.3, "pick": 0.3, "project": 2.5, "expand": 1.9, "combine": 1.2, "spread": 0.3}

time: 170 us -> 165 us (0.971)
  Pallas kernels: 168 us -> 163 us
    pallas_call x1, Pallas kernels: 168 us -> 163 us  [on_device(): pl.pallas_call(kernel, out_shape=jax.ShapeDtypeStruct((rows, width), jnp....]
where the time goes in v5:
time: 165 us; the launch traced here: 164 us
  Pallas kernels  163 us (99%)
    pallas_call x1, Pallas kernels, on_device(): pl.pallas_call(kernel, out_shape=jax.ShapeDtypeStruct((rows, width), jnp....  163 us

profile of v5, /device:TPU:1, one launch (start us, length us, event | category | flops | bytes accessed | tf_op | source)
XLA Modules:
  0.0 164.4 jit_solution(11745325897583865572)
XLA Ops:
  0.0 162.8 %shard_map.91 = bf16[16,4096]{1,0:T(8,128)(2,1)} custom-call(s32[8,16]{1,0:T(8,128)} %bitcast.2, f32[8,16]{1,0:T(8,128)} %bitcast.3, bf16[16,4096]{1,0:T(8,128)(2,1)} %x_ref.1, s32[192,128]{1,0:T(8,128)} %constant.6.clone.lane_hbm, f32[192,256]{1,0:T(8,128)} %constant.7.clone.code_hbm, f32[256,192]{1,0:T(8,128)} %constant.8.clone.code_t_hbm, ...), custom_call_target="tpu_custom_call" | custom-call | tf_op jit(solution)/shard_map/pallas_call | solution.py:649
  162.8 1.6 copy.11
